TPU v7x, 256 devices: a whole 4x4x8 slice. The times are simulated.
256 devices in a mesh: wide: 16 (over x_lo, y, core), narrow: 16 (over z, x_hi).
Axes of the slice: x: 4 (x_hi: 2, x_lo: 2; x = x_hi * 2 + x_lo), y: 4, z: 8, core: 2. Of those that a mesh axis runs over, the one named last changes fastest.
Arguments:
- coarse_basis: bfloat16 [32, 96, 3, 64, 8, 128], P('wide', None, None, 'narrow')
- material_ids: int32 [32, 64, 8, 128], P('wide', 'narrow'), may hold values from 0 to 15
- lame_table: bfloat16 [2, 16], replicated, may hold values from 0.5 to 4
- coarse_ids: int32 [32, 96], P('wide'), may hold values from 0 to 127, as said below
- coarse_slab: bfloat16 [98304, 2048], P('wide', 'narrow'), may hold values from -0.5 to 2.5, as said below
- panel_owner: int32 [1], replicated, may hold values from 0 to 14
Outputs:
- factored: bfloat16 [98304, 2048], P('wide', 'narrow')
- galerkin: float32 [32, 96, 96], P('wide')
Inputs may be any that keep to these rules, and one draw needn't show every extreme that they name: `coarse_ids`: the 96 numbers of a row are distinct. `coarse_slab`: for every column block t, the 128 x 128 block whose rows begin at t * 6144 is symmetric positive definite.
All inputs are finite; a program needn't handle non-finite values.
Results may differ from a plain program's by a relative error of at most 0.001.
The roundings to bfloat16 on the way count: a program that leaves them out, or rounds other values in their place, can miss the bound.
Values may be sent and summed in bfloat16 or wider, within the bound.
A program may use at most 192 MiB of HBM per device.

v0:
```python
import jax
import jax.numpy as jnp
from jax import lax
from jax.sharding import PartitionSpec as P


def padded_2(x, sides, width):
    for axis, dim in sides:
        count, length = (lax.axis_size(axis), x.shape[dim])
        up = [(i, (i + 1) % count) for i in range(count - 1)]
        down = [(j, i) for i, j in up]
        last = lax.slice_in_dim(x, length - width, length, axis=dim)
        initial = lax.slice_in_dim(x, 0, width, axis=dim)
        before = lax.ppermute(last, axis, up)
        after = lax.ppermute(initial, axis, down)
        x = jnp.concatenate([before, x, after], axis=dim)
    return x


def broadcast(value, axis, source):
    kept = jnp.where(lax.axis_index(axis) == source, value, 0).astype(value.dtype)
    return lax.psum(kept, axis)


def lower_inverse(lower):
    identity = jnp.eye(lower.shape[0], dtype=lower.dtype)
    return lax.linalg.triangular_solve(lower, identity, left_side=True, lower=True)


def lame_fields(material_ids, lame_table):
    values = lame_table.astype(jnp.float32)
    shear = jnp.zeros(material_ids.shape, jnp.float32)
    dilatation = jnp.zeros(material_ids.shape, jnp.float32)
    for material in range(values.shape[1]):
        chosen = material_ids == material
        shear = jnp.where(chosen, values[0, material], shear)
        dilatation = jnp.where(chosen, values[1, material], dilatation)
    return (shear, dilatation)


def shifted(field, axis, step):
    length = field.shape[axis]
    border = jnp.zeros_like(lax.slice_in_dim(field, 0, 1, axis=axis))
    if step > 0:
        return jnp.concatenate([lax.slice_in_dim(field, 1, length, axis=axis), border], axis=axis)
    return jnp.concatenate([border, lax.slice_in_dim(field, 0, length - 1, axis=axis)], axis=axis)


def face_weight(coeff_one, coeff_two, direction):
    shear = 0.5 * (coeff_one[:, 0:1] + coeff_two[:, 0:1])
    dilate = 0.5 * (coeff_one[:, 1:2] + coeff_two[:, 1:2])
    unit = (jnp.arange(3) == direction).astype(shear.dtype).reshape(1, 1, 3, 1, 1, 1)
    return shear + unit * (dilate + shear)


def operator_image(padded, coeff):
    centre = padded[:, :, :, 1:-1]
    coeff_centre = coeff[:, :, :, 1:-1]
    pairs = [
        (padded[:, :, :, 2:], coeff[:, :, :, 2:], 0),
        (padded[:, :, :, :-2], coeff[:, :, :, :-2], 0),
    ]
    for axis, direction in ((4, 1), (5, 2)):
        for step in (1, -1):
            pairs.append(
                (shifted(centre, axis, step), shifted(coeff_centre, axis, step), direction)
            )
    image = jnp.zeros(centre.shape, centre.dtype)
    for other, other_coeff, direction in pairs:
        image = image + face_weight(coeff_centre, other_coeff, direction) * (centre - other)
    return image


def galerkin_of(left_field, right_field):
    subs, funcs = (left_field.shape[0], left_field.shape[1])
    return jnp.einsum(
        "sak,sbk->sab",
        left_field.reshape(subs, funcs, -1),
        right_field.reshape(subs, funcs, -1),
        precision=lax.Precision.HIGHEST,
    )


def diagonal_factor(diagonal):
    diagonal = 0.5 * (diagonal + diagonal.T)
    lower = jnp.linalg.cholesky(diagonal)
    return (lower, lower_inverse(lower))


def panel_factor(column, lower, inverse, wide_index, owner, stride):
    solved = jnp.dot(column.astype(jnp.float32), inverse.T, precision=lax.Precision.HIGHEST)
    rows = lax.broadcasted_iota(jnp.int32, solved.shape, 0)
    head = rows < lower.shape[0]
    own_block = jnp.pad(lower, ((0, solved.shape[0] - lower.shape[0]), (0, 0)))
    diagonal_rows = head & (wide_index == owner * stride)
    earlier = head & (wide_index % stride == 0) & (wide_index // stride < owner)
    solved = jnp.where(diagonal_rows, own_block, solved)
    solved = jnp.where(earlier, 0.0, solved)
    return solved.astype(jnp.bfloat16)


def on_device(coarse_basis, material_ids, lame_table, coarse_ids, coarse_slab, panel_owner):
    narrow_count = lax.axis_size("narrow")
    stride = lax.axis_size("wide") // narrow_count
    wide_index = lax.axis_index("wide")
    narrow_index = lax.axis_index("narrow")
    owner = panel_owner[0]
    block = coarse_slab.shape[1]
    shear, dilatation = lame_fields(material_ids, lame_table)
    coeff = jnp.stack([shear, dilatation], 1)[:, :, None].astype(jnp.bfloat16)
    padded, coeff_padded = (
        padded_2(coarse_basis, (("narrow", 3),), 1),
        padded_2(coeff, (("narrow", 3),), 1),
    )
    padded = padded.astype(jnp.float32)
    image = operator_image(padded, coeff_padded.astype(jnp.float32))
    partial_sum = galerkin_of(padded[:, :, :, 1:-1], image)
    galerkin = lax.psum(partial_sum, "narrow")
    slots = (coarse_ids[:, :, None] == jnp.arange(block)[None, None, :]).astype(jnp.float32)
    spread = jnp.einsum("sab,sbc->sac", galerkin, slots, precision=lax.Precision.HIGHEST)
    added = jnp.einsum("sar,sac->rc", slots, spread, precision=lax.Precision.HIGHEST)
    assemble_here = (wide_index == narrow_index * stride) & (narrow_index >= owner)
    base = coarse_slab.astype(jnp.float32)
    base = base.at[:block].add(jnp.where(assemble_here, added, 0.0))
    diagonal = broadcast(base[:block], "wide", owner * stride)
    lower, inverse = diagonal_factor(diagonal)

    def owned():
        return panel_factor(coarse_slab, lower, inverse, wide_index, owner, stride)

    def empty_panel():
        return jnp.zeros(coarse_slab.shape, jnp.bfloat16)

    local_factor = lax.cond(narrow_index == owner, owned, empty_panel)
    factor = broadcast(local_factor, "narrow", owner)
    rows_needed = broadcast(factor[:block], "wide", narrow_index * stride)

    def updated():
        return base - jnp.einsum(
            "rk,ck->rc", factor, rows_needed, preferred_element_type=jnp.float32
        )

    def unchanged():
        return base

    result = lax.cond(narrow_index > owner, updated, unchanged)
    result = jnp.where(narrow_index == owner, factor.astype(jnp.float32), result)
    return (result.astype(jnp.bfloat16), galerkin)


def solution(mesh):
    return jax.shard_map(
        on_device,
        mesh=mesh,
        in_specs=(
            P("wide", None, None, "narrow", None, None),
            P("wide", "narrow", None, None),
            P(),
            P("wide", None),
            P("wide", "narrow"),
            P(),
        ),
        out_specs=(P("wide", "narrow"), P("wide", None, None)),
        check_vma=False,
    )
```

profile of v0, /device:TPU:32, one launch (start us, length us, event | category | flops | bytes accessed | tf_op | source)
XLA Modules:
  0.0 718.8 jit_solution(17513806060626854294)
XLA Ops:
  7.2 2.1 fusion.63
  9.3 1.8 fusion.64
  11.1 10.8 %select_convert_fusion.2 = (bf16[2,4,8,128]{3,2,1,0:T(8,128)(2,1)S(1)}, pred[2,4,8,128]{3,2,1,0:T(8,128)(4,1)S(1)}, pred[2,4,8,128]{3,2,1,0:T(8,128)(4,1)S(1)}, ...) fusion(bf16[]{:T(256)} %bitcast.16, ...), kind=kLoop, calls=%fused_computation.93 | loop fusion | flops 262144 | bytes 180256 | tf_op jit(solution)/shard_map/convert.7
  21.9 10.2 %select_convert_fusion.1 = bf16[2,4,8,128]{3,2,1,0:T(8,128)(2,1)S(1)} fusion(pred[2,4,8,128]{3,2,1,0:T(8,128)(4,1)S(1)} %get-tuple-element.65, pred[2,4,8,128]{3,2,1,0:T(8,128)(4,1)S(1)} %get-tuple-element.64, pred[2,4,8,128]{3,2,1,0:T(8,128)(4,1)S(1)} %get-tuple-element.63, pred[2,4,8,128]{3,2,1,0:T(8,128)(4,1)S(1)} %get-tuple-element.62, ...), kind=kLoop, calls=%fused_computation.92 | loop fusion | flops 131072 | bytes 147488 | tf_op jit(solution)/shard_map/convert.6
  32.7 4.9 collective-permute-start
  37.7 3.3 collective-permute-start.1
  41.0 2.1 fusion.60
  43.1 4.0 collective-permute-start.2
  47.1 4.2 collective-permute-start.3
  53.6 7.6 %reshape.222 = bf16[2,96,12288]{2,1,0:T(8,128)(2,1)} reshape(bf16[2,96,3,4,8,128]{5,4,3,2,1,0:T(8,128)(2,1)} %param.12) | data formatting | bytes 9437184 | tf_op jit(solution)/shard_map/reshape | solution.py:78
  63.7 33.3 %collective-permute-done.2 = bf16[2,96,3,1,8,128]{5,4,3,2,1,0:T(8,128)(2,1)S(1)} collective-permute-done((bf16[2,96,3,1,8,128]{5,4,3,2,1,0:T(8,128)(2,1)S(1)}, bf16[2,96,3,1,8,128]{5,4,3,2,1,0:T(8,128)(2,1)S(1)}, u32[]{:S(2)}, u32[]{:S(2)}) %collective-permute-start.2) | collective-permute-done | bytes 1179680 | tf_op jit(solution)/shard_map/ppermute | solution.py:14
  97.0 2.9 collective-permute-done.3
  99.9 9.3 %maximum_convert_fusion = f32[2,96,3,6,8,128]{5,4,3,2,1,0:T(8,128)} fusion(bf16[2,96,3,1,8,128]{5,4,3,2,1,0:T(8,128)(2,1)} %collective-permute-done.3, bf16[2,96,3,4,8,128]{5,4,3,2,1,0:T(8,128)(2,1)} %param.12, bf16[2,96,3,1,8,128]{5,4,3,2,1,0:T(8,128)(2,1)S(1)} %collective-permute-done.2), kind=kLoop, calls=%fused_computation.16 | loop fusion | flops 10616832 | bytes 21233664 | tf_op jit(solution)/shard_map/convert_element_type | solution.py:115
  109.2 14.4 %fusion.58 = (f32[2,96,3,4,7,128]{5,4,3,2,1,0:T(8,128)}, f32[2,96,3,4,7,128]{5,4,3,2,1,0:T(8,128)}) fusion(f32[2,96,3,6,8,128]{5,4,3,2,1,0:T(8,128)} %maximum_convert_fusion), kind=kLoop, calls=%fused_computation.123 | loop fusion | bytes 33030144 | tf_op jit(solution)/shard_map/slice | solution.py:45
  123.6 2.5 copy-done
  126.1 8.2 %fusion.59 = (f32[2,96,3,4,8,127]{5,4,3,2,1,0:T(8,128)}, f32[2,96,3,4,8,127]{5,4,3,2,1,0:T(8,128)}) fusion(f32[2,96,3,6,8,128]{5,4,3,2,1,0:T(8,128)S(1)} %copy-done), kind=kLoop, calls=%fused_computation.124 | loop fusion | bytes 37453824 | tf_op jit(solution)/shard_map/slice | solution.py:45
  134.3 27.3 %fusion.9 = f32[2,96,3,4,8,128]{5,4,3,2,1,0:T(8,128)} fusion(f32[2,96,3,6,8,128]{5,4,3,2,1,0:T(8,128)} %maximum_convert_fusion, f32[2,96,3,4,8,127]{5,4,3,2,1,0:T(8,128)} %get-tuple-element.71, f32[2,96,3,4,8,127]{5,4,3,2,1,0:T(8,128)} %get-tuple-element.70, f32[2,96,3,4,7,128]{5,4,3,2,1,0:T(8,128)} %get-tuple-element.69, ...), kind=kLoop, calls=%fused_computation.13 | loop fusion | flops 40108032 | bytes 73580544 | tf_op jit(solution)/shard_map/add | solution.py:70
  161.6 10.1 %reshape.221 = f32[2,96,12288]{2,1,0:T(8,128)} reshape(f32[2,96,3,4,8,128]{5,4,3,2,1,0:T(8,128)} %fusion.9) | data formatting | bytes 18874368 | tf_op jit(solution)/shard_map/reshape | solution.py:79
  171.7 10.1 %convolution_bitcast_fusion = f32[2,96,96]{1,2,0:T(8,128)} fusion(f32[2,96,12288]{2,1,0:T(8,128)} %reshape.221, bf16[2,96,12288]{2,1,0:T(8,128)(2,1)} %reshape.222), kind=kOutput, calls=%fused_computation.19 | convolution fusion | flops 2717908992 | bytes 14229504 | tf_op jit(solution)/shard_map/sak,sbk->sab/dot_general | solution.py:76
  182.5 1.6 convert_element_type.93
  184.1 159.0 %all-reduce.13.cloned.1.call-done = f32[2,96,96]{1,2,0:T(8,128)} async-done(((f32[2,96,96]{1,2,0:T(8,128)}), f32[2,96,96]{1,2,0:T(8,128)}) %all-reduce.13.cloned.1.call-update) | async-done | bytes 73744 | tf_op jit(solution)/shard_map/psum | solution.py:118
  343.1 1.2 fusion.13
  345.4 109.8 %all-reduce.15.cloned.1.call-done = f32[128,128]{1,0:T(8,128)} async-done(((f32[128,128]{1,0:T(8,128)}), f32[128,128]{1,0:T(8,128)}) %all-reduce.15.cloned.1.call-update) | async-done | bytes 65552 | tf_op jit(solution)/shard_map/psum | solution.py:22
  455.2 0.9 copy.8
  457.1 11.7 %cholesky.16 = f32[128,128]{1,0:T(8,128)S(1)} custom-call(f32[128,128]{1,0:T(8,128)S(1)} %fusion.16), custom_call_target="Cholesky" | custom-call | tf_op jit(solution)/shard_map/jit(cholesky)/cholesky | solution.py:86
  470.2 9.8 %custom-call.6 = f32[1,128,128]{1,2,0:T(8,128)S(1)} custom-call(f32[1,128,128]{2,1,0:T(8,128)S(1)} %get-tuple-element.47), custom_call_target="InvertDiagBlocksLowerTriangular" | custom-call | tf_op jit(solution)/shard_map/triangular_solve | solution.py:27
  480.2 1.4 conditional.2
  480.3 1.3 broadcast.208
  481.6 1.2 broadcast_select_fusion
  483.6 172.1 %all-reduce.17.cloned.1.call-done = bf16[6144,128]{1,0:T(8,128)(2,1)} async-done(((bf16[6144,128]{1,0:T(8,128)(2,1)}), bf16[6144,128]{1,0:T(8,128)(2,1)}) %all-reduce.17.cloned.1.call-update) | async-done | bytes 1572880 | tf_op jit(solution)/shard_map/psum | solution.py:22
  656.5 52.9 %psum.31 = bf16[128,128]{1,0:T(8,128)(2,1)S(1)} all-reduce(bf16[128,128]{1,0:T(8,128)(2,1)S(1)} %slice_select_fusion), channel_id=1, replica_groups=mesh['wide'=16,'narrow'=16] {'wide'}, use_global_device_ids=true, to_apply=%region_7.8 | all-reduce | flops 16384 | bytes 65536 | tf_op jit(solution)/shard_map/psum | solution.py:22
  709.4 2.9 select_convert_fusion
  (37 shorter events, 10.6 us)
Async XLA Ops:
  7.2 336.0 %all-reduce.13.cloned.1.call-start = ((), (), s32[]{:S(2)}) async-start(), calls=%async_computation | async-start | bytes 196608 | tf_op jit(solution)/shard_map/psum | solution.py:118
  32.7 28.5 %collective-permute-start = (bf16[2,2,1,1,8,128]{5,4,3,0,1,2:T(8,128)(2,1)}, bf16[2,2,1,1,8,128]{5,4,3,0,1,2:T(8,128)(2,1)S(1)}, u32[]{:S(2)}, u32[]{:S(2)}) collective-permute-start(bf16[2,2,1,1,8,128]{5,4,3,0,1,2:T(8,128)(2,1)} %get-tuple-element.96), channel_id=1, source_target_pairs={{0,1},{1,2},{2,3},{3,4},{4,5},{5,6},{6,7},{7,8},{8,9},{9,10},{10,1... | collective-permute-start | bytes 24584 | tf_op jit(solution)/shard_map/ppermute | solution.py:14
  37.7 23.5 %collective-permute-start.1 = (bf16[2,2,1,1,8,128]{5,4,3,0,1,2:T(8,128)(2,1)}, bf16[2,2,1,1,8,128]{5,4,3,0,1,2:T(8,128)(2,1)S(1)}, u32[]{:S(2)}, u32[]{:S(2)}) collective-permute-start(bf16[2,2,1,1,8,128]{5,4,3,0,1,2:T(8,128)(2,1)} %get-tuple-element.97), channel_id=1, source_target_pairs={{1,0},{2,1},{3,2},{4,3},{5,4},{6,5},{7,6},{8,7},{9,8},{10,9},{11,1... | collective-permute-start | bytes 24584 | tf_op jit(solution)/shard_map/ppermute | solution.py:15
  43.1 54.0 %collective-permute-start.2 = (bf16[2,96,3,1,8,128]{5,4,3,2,1,0:T(8,128)(2,1)S(1)}, bf16[2,96,3,1,8,128]{5,4,3,2,1,0:T(8,128)(2,1)S(1)}, u32[]{:S(2)}, u32[]{:S(2)}) collective-permute-start(bf16[2,96,3,1,8,128]{5,4,3,2,1,0:T(8,128)(2,1)S(1)} %get-tuple-element.72), channel_id=1, source_target_pairs={{0,1},{1,2},{2,3},{3,4},{4,5},{5,6},{6,7},{7,8},{8,9},{9,10},{10,1... | collective-permute-start | bytes 3538952 | tf_op jit(solution)/shard_map/ppermute | solution.py:14
  47.1 52.8 %collective-permute-start.3 = (bf16[2,96,3,1,8,128]{5,4,3,2,1,0:T(8,128)(2,1)S(1)}, bf16[2,96,3,1,8,128]{5,4,3,2,1,0:T(8,128)(2,1)}, u32[]{:S(2)}, u32[]{:S(2)}) collective-permute-start(bf16[2,96,3,1,8,128]{5,4,3,2,1,0:T(8,128)(2,1)S(1)} %get-tuple-element.73), channel_id=1, source_target_pairs={{1,0},{2,1},{3,2},{4,3},{5,4},{6,5},{7,6},{8,7},{9,8},{10,9},{11,1... | collective-permute-start | bytes 3538952 | tf_op jit(solution)/shard_map/ppermute | solution.py:15
  109.2 16.9 %copy-start = (f32[2,96,3,6,8,128]{5,4,3,2,1,0:T(8,128)S(1)}, f32[2,96,3,6,8,128]{5,4,3,2,1,0:T(8,128)}, u32[]{:S(2)}) copy-start(f32[2,96,3,6,8,128]{5,4,3,2,1,0:T(8,128)} %maximum_convert_fusion) | copy-start | bytes 42467332
  171.7 171.4 %copy-start.2 = (s32[2,96]{1,0:T(2,128)S(1)}, s32[2,96]{1,0:T(2,128)}, u32[]{:S(2)}) copy-start(s32[2,96]{1,0:T(2,128)} %param.15) | copy-start | bytes 2308
  181.8 273.4 %all-reduce.15.cloned.1.call-start = ((), (), s32[]{:S(2)}) async-start(), calls=%async_computation.1 | async-start | bytes 131072 | tf_op jit(solution)/shard_map/psum | solution.py:22
  345.4 310.3 %all-reduce.17.cloned.1.call-start = ((), (), s32[]{:S(2)}) async-start(), calls=%async_computation.2 | async-start | bytes 3145728 | tf_op jit(solution)/shard_map/psum | solution.py:22
  480.2 2.7 copy-start.1
Sparse Core Ops, SparseCore 0:
  181.9 161.1 all-reduce.12
  346.3 108.8 all-reduce.14
  483.0 172.6 all-reduce.16
where the time goes:
time: 720 us; the launch traced here: 719 us
  waiting for transfers between devices  477 us (66%)
  other arithmetic  93.7 us (13%)
  blocking collectives  52.9 us (7%)
  local copies, waits for them, and re-layouts  52 us (7%)
  starting transfers between devices  16.6 us (2%)
  between operations  14.6 us (2%)
  matrix products  11.9 us (2%)
    psum x2, waiting for transfers between devices, broadcast(): return lax.psum(kept, axis)  282 us
    psum x1, waiting for transfers between devices, on_device(): galerkin = lax.psum(partial_sum, 'narrow')  159 us
    psum x1, blocking collectives, broadcast(): return lax.psum(kept, axis)  52.9 us
    ppermute x2, waiting for transfers between devices, padded_2(): before = lax.ppermute(last, axis, up)  33.3 us
    add x1, other arithmetic, operator_image(): image + face_weight(coeff_centre, other_coeff, direction) * (centre - other)  27.3 us
    slice x4, local copies, waits for them, and re-layouts, shifted(): lax.slice_in_dim(field, 1, length, axis=axis)  22.7 us
    another operation x2, other arithmetic  21 us
  transfers between devices with their start and end apart: 7, of which 5 were waited for; matrix products, arithmetic and copies ran while one was open for 2% of the time, Pallas kernels for 0%

commit v1 on v0

v1 whole, which is shorter than its diff:
```python
import functools

import jax
import jax.numpy as jnp
from jax import lax
from jax.experimental import pallas as pl
from jax.experimental.pallas import tpu as pltpu
from jax.sharding import PartitionSpec as P

MESH = pl.DeviceIdType.MESH
F32, BF16 = jnp.float32, jnp.bfloat16
NT = (((1,), (1,)), ((), ()))
NN = (((1,), (0,)), ((), ()))
PIECE = 24


def exact_dot(a, b, dims):
    return lax.dot_general(a, b, dims, precision=lax.Precision.HIGHEST, preferred_element_type=F32)


def split2(x):
    hi = x.astype(BF16)
    return hi, (x - hi.astype(F32)).astype(BF16)


def shift_up(x, axis):
    index = lax.broadcasted_iota(jnp.int32, x.shape, axis)
    return jnp.where(index == 0, 0.0, pltpu.roll(x, 1, axis))


def shift_down(x, axis):
    size = x.shape[axis]
    index = lax.broadcasted_iota(jnp.int32, x.shape, axis)
    return jnp.where(index == size - 1, 0.0, pltpu.roll(x, size - 1, axis))


def gather_kernel(
    owner_ref, table_ref, ids_ref, basis_ref, mat_ref, slab_ref,
    own_ref, panel_ref,
    tiles, halo, mats, mat_halo, head, coef, coef_halo, natural, left, right, first, acc, late,
    pieces, landed, reduced, wide_in, chosen,
    load_sem, small_sem, halo_send, halo_recv, mat_send, mat_recv, rs_send, rs_recv,
    wide_send, wide_recv, own_send, own_recv, panel_send, panel_recv,
):
    w, n = lax.axis_index("wide"), lax.axis_index("narrow")
    count = lax.axis_size("narrow")
    funcs = basis_ref.shape[1]
    layers = basis_ref.shape[3]
    group = lambda d: lax.rem(n + d, count)
    across = lambda d: lax.rem(w + d, count)

    def load(sc):
        s, c = lax.div(sc, 3), lax.rem(sc, 3)
        return pltpu.make_async_copy(basis_ref.at[s, :, c], tiles.at[sc], load_sem.at[sc])

    def halo_copy(sc):
        s, c = lax.div(sc, 3), lax.rem(sc, 3)
        return pltpu.make_async_remote_copy(
            src_ref=basis_ref.at[s, :, c, layers - 1], dst_ref=halo.at[sc],
            send_sem=halo_send.at[sc], recv_sem=halo_recv.at[sc],
            device_id=(w, group(1)), device_id_type=MESH)

    mat_copy = pltpu.make_async_copy(mat_ref, mats, small_sem.at[0])
    head_copy = pltpu.make_async_copy(slab_ref.at[pl.ds(0, 128)], head, small_sem.at[1])
    mat_halo_copy = pltpu.make_async_remote_copy(
        src_ref=mat_ref.at[:, layers - 1], dst_ref=mat_halo, send_sem=mat_send, recv_sem=mat_recv,
        device_id=(w, group(1)), device_id_type=MESH)

    mat_copy.start()
    for sc in range(6):
        load(sc).start()
    head_copy.start()

    barrier = pltpu.get_barrier_semaphore()

    def greet(d, carry):
        pl.semaphore_signal(barrier, inc=1, device_id=(w, group(d)), device_id_type=MESH)
        pl.semaphore_signal(barrier, inc=1, device_id=(across(d), n), device_id_type=MESH)
        return carry

    lax.fori_loop(1, count, greet, 0)
    pl.semaphore_wait(barrier, 2 * (count - 1))

    mat_halo_copy.start()
    for sc in range(6):
        halo_copy(sc).start()

    acc[...] = jnp.zeros_like(acc)
    late[...] = jnp.zeros_like(late)
    right[...] = jnp.zeros_like(right)
    pieces[...] = jnp.zeros_like(pieces)

    table = table_ref[...].astype(F32)
    mat_copy.wait()
    mat_halo_copy.wait()
    bottom = jnp.where(n == 0, 0.0, 1.0)
    top = jnp.where(n == count - 1, 1.0, 0.0)

    def lame(material):
        shear = jnp.zeros(material.shape, F32)
        dilate = jnp.zeros(material.shape, F32)
        for k in range(table.shape[1]):
            hit = material == k
            shear = jnp.where(hit, table[0:1, k:k + 1], shear)
            dilate = jnp.where(hit, table[1:2, k:k + 1], dilate)
        return shear, dilate

    for s in range(2):
        below = [x * bottom for x in lame(mat_halo[s])]
        cells = [lame(mats[s, i]) for i in range(layers)]
        for i in range(layers):
            here = cells[i]
            lower_x = below if i == 0 else cells[i - 1]

            def weights(other):
                m = 0.5 * (here[0] + other[0])
                return m, m + (m + 0.5 * (here[1] + other[1]))

            x_low = weights(lower_x)
            if i + 1 < layers:
                x_high = weights(cells[i + 1])
            else:
                x_high = [x * top for x in weights((jnp.zeros_like(here[0]),) * 2)]
            y_low = weights([shift_up(x, 0) for x in here])
            y_high = weights([shift_down(x, 0) for x in here])
            z_low = weights([shift_up(x, 1) for x in here])
            z_high = weights([shift_down(x, 1) for x in here])
            lane = lax.broadcasted_iota(jnp.int32, here[0].shape, 1)
            for c in range(3):
                px, py, pz = (int(c == d) for d in range(3))
                coef[3 * s + c, i, 0] = (x_low[px] + x_high[px]) + (y_low[py] + y_high[py]) + (z_low[pz] + z_high[pz])
                coef[3 * s + c, i, 1] = x_low[px]
                coef[3 * s + c, i, 2] = y_low[py]
                coef[3 * s + c, i, 3] = jnp.where(lane == 0, 0.0, z_low[pz])
                coef[3 * s + c, i, 4] = jnp.where(lane == lane.shape[1] - 1, 0.0, z_high[pz])
                if i == 0:
                    coef_halo[3 * s + c] = x_low[px] * bottom

    rows_y = 8

    def interior(sc, carry):
        s = lax.div(sc, 3)
        load(sc).wait()
        for i in range(layers):
            natural[i] = tiles[sc, :, i].astype(F32).reshape(funcs * rows_y, 128)

        def field(i, y):
            return natural[i, pl.ds(y, funcs, stride=rows_y), :]

        def k(i, which, y):
            return coef[sc, i, which, pl.ds(y, 1), :]

        for i in range(layers):
            for y in range(rows_y):
                v = field(i, y)
                image = k(i, 0, y) * v
                if i > 0:
                    image = image - k(i, 1, y) * field(i - 1, y)
                if i + 1 < layers:
                    image = image - k(i + 1, 1, y) * field(i + 1, y)
                if y > 0:
                    image = image - k(i, 2, y) * field(i, y - 1)
                if y + 1 < rows_y:
                    image = image - k(i, 2, y + 1) * field(i, y + 1)
                image = image - k(i, 3, y) * pltpu.roll(v, 1, 1) - k(i, 4, y) * pltpu.roll(v, 127, 1)
                lanes = slice(128 * y, 128 * (y + 1))
                hi, lo = split2(image)
                vb = v.astype(BF16)
                left[:, lanes] = vb
                if i == 0:
                    first[sc, :, lanes] = vb
                right[0:funcs, lanes] = hi
                right[128:128 + funcs, lanes] = lo
            acc[s] += lax.dot_general(left[...], right[...], NT, preferred_element_type=F32)
        return carry

    lax.fori_loop(0, 6, interior, 0)

    def boundary(sc, carry):
        s = lax.div(sc, 3)
        halo_copy(sc).wait()
        natural[0] = halo[sc].astype(F32).reshape(funcs * rows_y, 128)
        for y in range(rows_y):
            h = natural[0, pl.ds(y, funcs, stride=rows_y), :]
            hi, lo = split2(coef_halo[sc, pl.ds(y, 1), :] * h)
            lanes = slice(128 * y, 128 * (y + 1))
            left[:, lanes] = h.astype(BF16)
            right[0:funcs, lanes] = hi
            right[128:128 + funcs, lanes] = lo
        late[s, 0:funcs] += lax.dot_general(left[...], right[...], NT, preferred_element_type=F32)
        late[s, funcs:2 * funcs] += lax.dot_general(first[sc], right[...], NT, preferred_element_type=F32)
        return carry

    lax.fori_loop(0, 6, boundary, 0)

    head_copy.wait()
    mine = jnp.where(owner_ref[0] == n, 1.0, 0.0)
    for q in range(16):
        pieces[q, 16:24, :] = head[8 * q:8 * (q + 1), :].astype(F32) * mine
    for s in range(2):
        both = acc[s] + late[s, 0:funcs]
        total = both[:, 0:128] + both[:, 128:256]
        cross = late[s, funcs:2 * funcs, 0:128] + late[s, funcs:2 * funcs, 128:256]
        square = jnp.concatenate([cross, jnp.zeros((128 - funcs, 128), F32)], 0)
        total = total - cross - square.T[0:funcs]
        for z in range(8):
            pieces[2 * z + s, 0:12, :] = total[12 * z:12 * (z + 1), :]

    def rs_copy(d):
        return pltpu.make_async_remote_copy(
            src_ref=pieces.at[group(d)], dst_ref=landed.at[n], send_sem=rs_send.at[d], recv_sem=rs_recv.at[d],
            device_id=(w, group(d)), device_id_type=MESH)

    def wide_copy(d):
        return pltpu.make_async_remote_copy(
            src_ref=reduced, dst_ref=wide_in.at[w], send_sem=wide_send.at[d], recv_sem=wide_recv.at[d],
            device_id=(across(d), n), device_id_type=MESH)

    def own_copy(d):
        return pltpu.make_async_remote_copy(
            src_ref=reduced, dst_ref=own_ref.at[n], send_sem=own_send.at[d], recv_sem=own_recv.at[d],
            device_id=(w, group(d)), device_id_type=MESH)

    def panel_copy(d):
        return pltpu.make_async_remote_copy(
            src_ref=chosen, dst_ref=panel_ref.at[n], send_sem=panel_send.at[d], recv_sem=panel_recv.at[d],
            device_id=(w, group(d)), device_id_type=MESH)

    def start_all(copy):
        lax.fori_loop(1, count, lambda d, carry: (copy(d).start(), carry)[1], 0)

    def wait_all(copy):
        lax.fori_loop(1, count, lambda d, carry: (copy(d).wait(), carry)[1], 0)

    start_all(rs_copy)
    landed[n] = pieces[n]
    wait_all(rs_copy)
    total = landed[0]
    for q in range(1, 16):
        total = total + landed[q]
    reduced[...] = total
    reduced[12:14, :] = jnp.full((2, 128), -1.0, F32)
    reduced[12:14, 0:funcs] = ids_ref[...].astype(F32)
    start_all(wide_copy)
    start_all(own_copy)
    own_ref[n] = reduced[...]
    wide_in[w] = reduced[...]
    wait_all(wide_copy)
    chosen[...] = wide_in[owner_ref[0]]
    start_all(panel_copy)
    panel_ref[n] = chosen[...]
    wait_all(own_copy)
    wait_all(panel_copy)


def gather(owner, table, ids, basis, mat, slab):
    subs, funcs, comps, layers, rows_y, depth = basis.shape
    vmem, anyspace = pl.BlockSpec(memory_space=pltpu.VMEM), pl.BlockSpec(memory_space=pl.ANY)
    dma = pltpu.SemaphoreType.DMA
    piece = jax.ShapeDtypeStruct((16, PIECE, 128), F32)
    return pl.pallas_call(
        gather_kernel,
        out_shape=(piece, piece),
        in_specs=[pl.BlockSpec(memory_space=pltpu.SMEM), vmem, vmem, anyspace, anyspace, anyspace],
        out_specs=(vmem, vmem),
        scratch_shapes=[
            pltpu.VMEM((6, funcs, layers, rows_y, depth), BF16),
            pltpu.VMEM((6, funcs, rows_y, depth), BF16),
            pltpu.VMEM((subs, layers, rows_y, depth), jnp.int32),
            pltpu.VMEM((subs, rows_y, depth), jnp.int32),
            pltpu.VMEM((128, 128), BF16),
            pltpu.VMEM((6, layers, 5, rows_y, depth), F32),
            pltpu.VMEM((6, rows_y, depth), F32),
            pltpu.VMEM((layers, funcs * rows_y, depth), F32),
            pltpu.VMEM((funcs, rows_y * depth), BF16),
            pltpu.VMEM((256, rows_y * depth), BF16),
            pltpu.VMEM((6, funcs, rows_y * depth), BF16),
            pltpu.VMEM((subs, funcs, 256), F32),
            pltpu.VMEM((subs, 2 * funcs, 256), F32),
            pltpu.VMEM((16, PIECE, 128), F32),
            pltpu.VMEM((16, PIECE, 128), F32),
            pltpu.VMEM((PIECE, 128), F32),
            pltpu.VMEM((16, PIECE, 128), F32),
            pltpu.VMEM((PIECE, 128), F32),
            dma((6,)), dma((2,)), dma((6,)), dma((6,)), dma, dma,
            dma((16,)), dma((16,)), dma((16,)), dma((16,)), dma((16,)), dma((16,)), dma((16,)), dma((16,)),
        ],
        compiler_params=pltpu.CompilerParams(collective_id=0, has_side_effects=True, vmem_limit_bytes=56 << 20),
        name="galerkin_gather",
    )(owner, table, ids, basis, mat, slab)


def panel_kernel(owner_ref, panel_ref, own_ref, column_ref, rows_ref, slab_ref, out_ref, galerkin_ref, block, added_own, lower, parts, rows_bf):
    w, n = lax.axis_index("wide"), lax.axis_index("narrow")
    owner = owner_ref[0]
    funcs = galerkin_ref.shape[1]
    height, tile = out_ref.shape[0], 512

    def slots(pieces_ref, s):
        ids = pieces_ref[0, 12 + s:13 + s, :]
        index = lax.broadcasted_iota(jnp.int32, (128, 128), 0).astype(F32)
        return jnp.where(index == ids, 1.0, 0.0)

    def added_of(pieces_ref):
        total = jnp.zeros((128, 128), F32)
        for s in range(2):
            place = slots(pieces_ref, s)
            for z in range(8):
                block[12 * z:12 * (z + 1), :] = pieces_ref[2 * z + s, 0:12, :]
            total = total + exact_dot(exact_dot(place, block[...], NN), place, NT)
        return total

    block[...] = jnp.zeros_like(block)
    for s in range(2):
        for z in range(8):
            galerkin_ref[s, 12 * z:12 * (z + 1), :] = own_ref[2 * z + s, 0:12, 0:funcs]

    diagonal = added_of(panel_ref) + jnp.concatenate([panel_ref[q, 16:24, :] for q in range(16)], 0)
    diagonal = 0.5 * (diagonal + diagonal.T)
    sub = lax.broadcasted_iota(jnp.int32, (8, 128), 0)
    lane = lax.broadcasted_iota(jnp.int32, (8, 128), 1)
    a = [diagonal[8 * b:8 * (b + 1)] for b in range(16)]
    m = [jnp.where(lane == sub + 8 * b, 1.0, 0.0) for b in range(16)]
    for j in range(128):
        b0, r = divmod(j, 8)
        row_a, row_m = a[b0][r:r + 1], m[b0][r:r + 1]
        inverse = 1.0 / row_a[:, j:j + 1]
        row_a, row_m = row_a * inverse, row_m * inverse
        for b in range(b0, 16):
            if b == b0 and r == 7:
                continue
            f = a[b][:, j:j + 1]
            if b == b0:
                f = jnp.where(sub[:, 0:1] > r, f, 0.0)
            a[b] = a[b] - f * row_a
            m[b] = m[b] - f * row_m
    upper = []
    for b in range(16):
        on_diagonal = lane == sub + 8 * b
        d = jnp.sum(jnp.where(on_diagonal, a[b], 0.0), axis=1, keepdims=True)
        scale = lax.rsqrt(d)
        upper.append(jnp.where(lane >= sub + 8 * b, a[b] * scale, 0.0))
        m[b] = m[b] * scale
    lower[...] = jnp.concatenate(upper, 0).T
    inverse = jnp.concatenate(m, 0)
    hi, rest = split2(inverse)
    mid, low = split2(inverse - hi.astype(F32))
    parts[0:128] = hi
    parts[128:256] = mid
    parts[256:384] = low

    def solve(x):
        y = lax.dot_general(x, parts[...], NT, preferred_element_type=F32)
        return y[:, 0:128] + (y[:, 128:256] + y[:, 256:384])

    rows_bf[...] = solve(rows_ref[...]).astype(BF16)
    added_own[...] = jnp.zeros_like(added_own)

    @pl.when((w == n) & (n >= owner))
    def _():
        added_own[...] = added_of(own_ref)

    def store(start, size, factor, base):
        part = pl.ds(start, size)

        @pl.when(n > owner)
        def _():
            update = lax.dot_general(factor, rows_bf[...], NT, preferred_element_type=F32)
            out_ref[part, :] = (base - update).astype(BF16)

        @pl.when(n == owner)
        def _():
            out_ref[part, :] = factor

        @pl.when(n < owner)
        def _():
            out_ref[part, :] = base.astype(BF16)

    solved = solve(column_ref[0:128, :])
    solved = jnp.where(w == owner, lower[...], solved)
    solved = jnp.where(w < owner, 0.0, solved)
    store(0, 128, solved.astype(BF16), slab_ref[0:128, :].astype(F32) + added_own[...])

    def body(t, carry):
        start = pl.multiple_of(128 + t * tile, 128)
        part = pl.ds(start, tile)
        store(start, tile, solve(column_ref[part, :]).astype(BF16), slab_ref[part, :].astype(F32))
        return carry

    steps = (height - 128) // tile
    lax.fori_loop(0, steps, body, 0)
    done = 128 + steps * tile
    rest = slice(done, height)
    store(done, height - done, solve(column_ref[rest, :]).astype(BF16), slab_ref[rest, :].astype(F32))


def panel_step(owner, panel, own, column, rows, slab, funcs):
    vmem = pl.BlockSpec(memory_space=pltpu.VMEM)
    return pl.pallas_call(
        panel_kernel,
        out_shape=(jax.ShapeDtypeStruct(slab.shape, BF16), jax.ShapeDtypeStruct((2, funcs, funcs), F32)),
        in_specs=[pl.BlockSpec(memory_space=pltpu.SMEM)] + [vmem] * 5,
        out_specs=(vmem, vmem),
        scratch_shapes=[
            pltpu.VMEM((128, 128), F32), pltpu.VMEM((128, 128), F32), pltpu.VMEM((128, 128), F32),
            pltpu.VMEM((384, 128), BF16), pltpu.VMEM((128, 128), BF16),
        ],
        compiler_params=pltpu.CompilerParams(vmem_limit_bytes=48 << 20),
        name="panel_step",
    )(owner, panel, own, column, rows, slab)


def on_device(coarse_basis, material_ids, lame_table, coarse_ids, coarse_slab, panel_owner):
    w, n = lax.axis_index("wide"), lax.axis_index("narrow")
    column = lax.psum(jnp.where(n == panel_owner[0], coarse_slab, 0).astype(BF16), "narrow")
    rows = lax.psum(jnp.where(w == n, column[:128], 0).astype(BF16), "wide")
    own, panel = gather(panel_owner, lame_table, coarse_ids, coarse_basis, material_ids, coarse_slab)
    return panel_step(panel_owner, panel, own, column, rows, coarse_slab, coarse_basis.shape[1])


def solution(mesh):
    return jax.shard_map(
        on_device,
        mesh=mesh,
        in_specs=(
            P("wide", None, None, "narrow", None, None),
            P("wide", "narrow", None, None),
            P(),
            P("wide", None),
            P("wide", "narrow"),
            P(),
        ),
        out_specs=(P("wide", "narrow"), P("wide", None, None)),
        check_vma=False,
    )
```

time: 720 us -> 281 us (0.39)
  waiting for transfers between devices: 477 us -> 125 us
  other arithmetic: 93.7 us -> 2.02 us
  Pallas kernels: 0 us -> 83.2 us
  local copies, waits for them, and re-layouts: 52 us -> 3.27 us
  starting transfers between devices: 16.6 us -> 0.04 us
  matrix products: 11.9 us -> 0 us
    psum x3 -> x1, waiting for transfers between devices: 441 us -> 125 us  [on_device(): lax.psum(jnp.where(n == panel_owner[0], coarse_slab, 0).astype(BF16), 'na...]
    pallas_call x0 -> x2, Pallas kernels: none -> 83.2 us  [the longest x1 66.8 us: gather(): pl.pallas_call(gather_kernel, out_shape=(piece, piece), in_specs=[pl.Bloc...]
    another operation x7 -> x0, other arithmetic: 43.9 us -> none
    ppermute x4 -> x0, waiting for transfers between devices: 36.2 us -> none  [the longest x2 33.3 us: padded_2(): before = lax.ppermute(last, axis, up)]
    add x5 -> x0, other arithmetic: 28.9 us -> none  [the longest x1 27.3 us: operator_image(): image + face_weight(coeff_centre, other_coeff, direction) * (centre - other)]
    slice x7 -> x0, local copies, waits for them, and re-layouts: 28.6 us -> none  [the longest x4 22.7 us: shifted(): lax.slice_in_dim(field, 1, length, axis=axis)]
    reshape x2 -> x0, local copies, waits for them, and re-layouts: 17.7 us -> none  [the longest x1 10.1 us: galerkin_of(): right_field.reshape(subs, funcs, -1)]
    ppermute x4 -> x0, starting transfers between devices: 16.5 us -> none  [the longest x2 8.95 us: padded_2(): before = lax.ppermute(last, axis, up)]
  transfers between devices with their start and end apart: 7 -> 1, of which waited for: 5 -> 1; matrix products, arithmetic and copies ran while one was open for 2% -> 0% of each run, Pallas kernels for 0% -> 24%
where the time goes in v1:
time: 281 us
  waiting for transfers between devices  125 us (44%)
  Pallas kernels  83.2 us (30%)
  blocking collectives  52.9 us (19%)
  between operations  14.7 us (5%)
  local copies, waits for them, and re-layouts  3.27 us (1%)
    psum x1, waiting for transfers between devices, on_device(): lax.psum(jnp.where(n == panel_owner[0], coarse_slab, 0).astype(BF16), 'na...  125 us
    pallas_call x1, Pallas kernels, gather(): pl.pallas_call(gather_kernel, out_shape=(piece, piece), in_specs=[pl.Bloc...  66.8 us
    psum x1, blocking collectives, on_device(): rows = lax.psum(jnp.where(w == n, column[:128], 0).astype(BF16), 'wide')  52.9 us
    pallas_call x1, Pallas kernels, panel_step(): pl.pallas_call(panel_kernel, out_shape=(jax.ShapeDtypeStruct(slab.shape,...  16.4 us
  transfers between devices with their start and end apart: 1, of which 1 were waited for; matrix products, arithmetic and copies ran while one was open for 0% of the time, Pallas kernels for 24%

profile of v1, /device:TPU:32, one launch (start us, length us, event | category | flops | bytes accessed | tf_op | source)
XLA Modules:
  0.0 281.1 jit_solution(14640050929672432889)
XLA Ops:
  7.2 0.0 all-reduce.2.cloned.1.call-start
  7.9 1.3 broadcast_select_fusion
  9.1 0.0 all-reduce.2.cloned.1.call-update
  9.2 0.0 copy-start
  9.2 66.8 %galerkin_gather.1 = (f32[16,24,128]{2,1,0:T(8,128)}, f32[16,24,128]{2,1,0:T(8,128)}) custom-call(s32[1]{0:T(128)} %copy.9.owner_ref, bf16[2,16]{1,0:T(2,128)(2,1)} %table_ref.1, s32[2,96]{1,0:T(2,128)} %ids_ref.1, bf16[2,96,3,4,8,128]{5,4,3,2,1,0:T(8,128)(2,1)} %basis_ref.1, s32[2,4,8,128]{3,2,1,0:T(8,128)} %mat_ref.1, bf16[6144,128]{1,0:T(8,128)(2,1)} %slab_ref.3), custom_call_target="tpu_custom_call" | custom-call | tf_op jit(solution)/shard_map/galerkin_gather/pallas_call | solution.py:261
  75.9 125.0 %all-reduce.2.cloned.1.call-done.column_ref = bf16[6144,128]{1,0:T(8,128)(2,1)} async-done(((bf16[6144,128]{1,0:T(8,128)(2,1)}), bf16[6144,128]{1,0:T(8,128)(2,1)}) %all-reduce.2.cloned.1.call-update) | async-done | bytes 1572880 | tf_op jit(solution)/shard_map/psum | solution.py:415
  200.9 0.8 slice_select_fusion
  201.7 52.9 %psum.15.rows_ref = bf16[128,128]{1,0:T(8,128)(2,1)S(1)} all-reduce(bf16[128,128]{1,0:T(8,128)(2,1)S(1)} %slice_select_fusion), channel_id=1, replica_groups=mesh['wide'=16,'narrow'=16] {'wide'}, use_global_device_ids=true, to_apply=%region_1.2 | all-reduce | flops 16384 | bytes 65536 | tf_op jit(solution)/shard_map/psum | solution.py:416
  254.6 0.0 copy-done
  254.6 0.0 copy-start.1
  254.6 1.4 copy-done.1
  256.0 0.0 copy-start.2
  256.0 0.9 copy-done.2
  257.0 0.0 copy-start.3
  257.0 0.9 copy-done.3
  257.9 16.4 %panel_step.1 = (bf16[6144,128]{1,0:T(8,128)(2,1)}, f32[2,96,96]{2,1,0:T(8,128)}) custom-call(s32[1]{0:T(128)} %copy.9.owner_ref, f32[16,24,128]{2,1,0:T(8,128)S(1)} %copy-done.3, f32[16,24,128]{2,1,0:T(8,128)S(1)} %copy-done.2, bf16[6144,128]{1,0:T(8,128)(2,1)S(1)} %copy-done.1, bf16[128,128]{1,0:T(8,128)(2,1)S(1)} %psum.15.rows_ref, ...), custom_call_target="tpu_custom_call" | custom-call | tf_op jit(solution)/shard_map/panel_step/pallas_call | solution.py:399
Async XLA Ops:
  7.2 193.8 %all-reduce.2.cloned.1.call-start = ((), (), s32[]{:S(2)}) async-start(), calls=%async_computation | async-start | bytes 3145728 | tf_op jit(solution)/shard_map/psum | solution.py:415
  9.2 245.5 %copy-start = (bf16[6144,128]{1,0:T(8,128)(2,1)S(1)}, bf16[6144,128]{1,0:T(8,128)(2,1)}, u32[]{:S(2)}) copy-start(bf16[6144,128]{1,0:T(8,128)(2,1)} %slab_ref.3) | copy-start | bytes 4718596
  254.6 1.4 copy-start.1
  256.0 0.9 copy-start.2
  257.0 0.9 copy-start.3
Sparse Core Ops, SparseCore 0:
  11.2 189.7 all-reduce.1

commit v2 on v1

--- a/solution.py
+++ b/solution.py
@@ -12,6 +12,9 @@
 NT = (((1,), (1,)), ((), ()))
 NN = (((1,), (0,)), ((), ()))
 PIECE = 24
+WIDER = 32
+STREAMS = 4
+RING = 8
 
 
 def exact_dot(a, b, dims):
@@ -36,11 +39,12 @@
 
 def gather_kernel(
     owner_ref, table_ref, ids_ref, basis_ref, mat_ref, slab_ref,
-    own_ref, panel_ref,
-    tiles, halo, mats, mat_halo, head, coef, coef_halo, natural, left, right, first, acc, late,
-    pieces, landed, reduced, wide_in, chosen,
+    own_ref, panel_ref, column_ref,
+    tiles, halo, mats, mat_halo, coef, coef_halo, natural, left, right, first, acc, late,
+    pieces, landed, reduced, wide_in, chosen, slab, passing, swapped,
     load_sem, small_sem, halo_send, halo_recv, mat_send, mat_recv, rs_send, rs_recv,
     wide_send, wide_recv, own_send, own_recv, panel_send, panel_recv,
+    ring_send, ring_recv, swap_send, swap_recv, spread_send, spread_recv,
 ):
     w, n = lax.axis_index("wide"), lax.axis_index("narrow")
     count = lax.axis_size("narrow")
@@ -60,16 +64,56 @@
             send_sem=halo_send.at[sc], recv_sem=halo_recv.at[sc],
             device_id=(w, group(1)), device_id_type=MESH)
 
+    z, half = lax.div(n, 2), lax.rem(n, 2)
+    piece_rows = column_ref.shape[0] // RING
+    chunk = piece_rows // STREAMS
+    way = lambda t: 1 if t % 2 == 0 else RING - 1
+    beside = lambda t: 2 * lax.rem(z + way(t), RING) + half
+    piece_at = lambda t, k: lax.rem(z + (RING - way(t)) * k, RING)
+
+    def chunk_rows(t, piece):
+        return pl.ds(pl.multiple_of(piece * piece_rows + t * chunk, chunk), chunk)
+
+    def ring_copy(t, k, source=None):
+        return pltpu.make_async_remote_copy(
+            src_ref=passing.at[t, k - 1] if source is None else source, dst_ref=passing.at[t, k],
+            send_sem=ring_send.at[t, k], recv_sem=ring_recv.at[t, k],
+            device_id=(w, beside(t)), device_id_type=MESH)
+
+    def ring_start(t):
+        ring_copy(t, 0, slab.at[chunk_rows(t, piece_at(t, 1))]).start()
+
+    def ring_land(t, k):
+        ring_copy(t, k, passing.at[t, k]).wait()
+        passing[t, k] += slab[chunk_rows(t, piece_at(t, k + 2)), :]
+
+    def swap_copy(t):
+        return pltpu.make_async_remote_copy(
+            src_ref=passing.at[t, RING - 2], dst_ref=swapped.at[t], send_sem=swap_send.at[t], recv_sem=swap_recv.at[t],
+            device_id=(w, n + 1 - 2 * half), device_id_type=MESH)
+
+    def spread_copy(t, k):
+        part = column_ref.at[chunk_rows(t, piece_at(t, k))]
+        return pltpu.make_async_remote_copy(
+            src_ref=part, dst_ref=part, send_sem=spread_send.at[t, k], recv_sem=spread_recv.at[t, k],
+            device_id=(w, beside(t)), device_id_type=MESH)
+
+    def spread_step(k):
+        for t in range(STREAMS):
+            spread_copy(t, k).wait()
+            if k + 1 < RING - 1:
+                spread_copy(t, k + 1).start()
+
     mat_copy = pltpu.make_async_copy(mat_ref, mats, small_sem.at[0])
-    head_copy = pltpu.make_async_copy(slab_ref.at[pl.ds(0, 128)], head, small_sem.at[1])
+    slab_copy = pltpu.make_async_copy(slab_ref, slab, small_sem.at[1])
     mat_halo_copy = pltpu.make_async_remote_copy(
         src_ref=mat_ref.at[:, layers - 1], dst_ref=mat_halo, send_sem=mat_send, recv_sem=mat_recv,
         device_id=(w, group(1)), device_id_type=MESH)
 
+    slab_copy.start()
     mat_copy.start()
     for sc in range(6):
         load(sc).start()
-    head_copy.start()
 
     barrier = pltpu.get_barrier_semaphore()
 
@@ -79,11 +123,22 @@
         return carry
 
     lax.fori_loop(1, count, greet, 0)
+    mine = jnp.where(owner_ref[0] == n, 1.0, 0.0).astype(BF16)
+    slab_copy.wait()
+
+    def mask(q, carry):
+        part = pl.ds(pl.multiple_of(q * piece_rows, piece_rows), piece_rows)
+        slab[part, :] = slab[part, :] * mine
+        return carry
+
+    lax.fori_loop(0, RING, mask, 0)
     pl.semaphore_wait(barrier, 2 * (count - 1))
 
     mat_halo_copy.start()
     for sc in range(6):
         halo_copy(sc).start()
+    for t in range(STREAMS):
+        ring_start(t)
 
     acc[...] = jnp.zeros_like(acc)
     late[...] = jnp.zeros_like(late)
@@ -172,9 +227,18 @@
                 right[0:funcs, lanes] = hi
                 right[128:128 + funcs, lanes] = lo
             acc[s] += lax.dot_general(left[...], right[...], NT, preferred_element_type=F32)
+            ring_land(i, sc)
+            ring_copy(i, sc + 1).start()
         return carry
 
     lax.fori_loop(0, 6, interior, 0)
+    for t in range(STREAMS):
+        ring_land(t, RING - 2)
+        swap_copy(t).start()
+    for t in range(STREAMS):
+        swap_copy(t).wait()
+        column_ref[chunk_rows(t, z), :] = passing[t, RING - 2] + swapped[t]
+        spread_copy(t, 0).start()
 
     def boundary(sc, carry):
         s = lax.div(sc, 3)
@@ -191,20 +255,21 @@
         late[s, funcs:2 * funcs] += lax.dot_general(first[sc], right[...], NT, preferred_element_type=F32)
         return carry
 
-    lax.fori_loop(0, 6, boundary, 0)
-
-    head_copy.wait()
-    mine = jnp.where(owner_ref[0] == n, 1.0, 0.0)
+    lax.fori_loop(0, 3, boundary, 0)
+    spread_step(0)
+    lax.fori_loop(3, 6, boundary, 0)
+
+    head = slab[0:128, :].astype(F32)
     for q in range(16):
-        pieces[q, 16:24, :] = head[8 * q:8 * (q + 1), :].astype(F32) * mine
+        pieces[q, 16:24, :] = head[8 * q:8 * (q + 1), :]
     for s in range(2):
         both = acc[s] + late[s, 0:funcs]
         total = both[:, 0:128] + both[:, 128:256]
         cross = late[s, funcs:2 * funcs, 0:128] + late[s, funcs:2 * funcs, 128:256]
         square = jnp.concatenate([cross, jnp.zeros((128 - funcs, 128), F32)], 0)
         total = total - cross - square.T[0:funcs]
-        for z in range(8):
-            pieces[2 * z + s, 0:12, :] = total[12 * z:12 * (z + 1), :]
+        for part in range(RING):
+            pieces[2 * part + s, 0:12, :] = total[12 * part:12 * (part + 1), :]
 
     def rs_copy(d):
         return pltpu.make_async_remote_copy(
@@ -223,7 +288,7 @@
 
     def panel_copy(d):
         return pltpu.make_async_remote_copy(
-            src_ref=chosen, dst_ref=panel_ref.at[n], send_sem=panel_send.at[d], recv_sem=panel_recv.at[d],
+            src_ref=chosen.at[group(d)], dst_ref=panel_ref.at[n], send_sem=panel_send.at[d], recv_sem=panel_recv.at[d],
             device_id=(w, group(d)), device_id_type=MESH)
 
     def start_all(copy):
@@ -234,6 +299,8 @@
 
     start_all(rs_copy)
     landed[n] = pieces[n]
+    spread_step(1)
+    spread_step(2)
     wait_all(rs_copy)
     total = landed[0]
     for q in range(1, 16):
@@ -245,10 +312,16 @@
     start_all(own_copy)
     own_ref[n] = reduced[...]
     wide_in[w] = reduced[...]
+    spread_step(3)
     wait_all(wide_copy)
-    chosen[...] = wide_in[owner_ref[0]]
+    of_owner = wide_in[owner_ref[0]]
+    for q in range(16):
+        chosen[q, 0:24, :] = of_owner
+        chosen[q, 24:32, :] = wide_in[q, 16:24, :]
     start_all(panel_copy)
-    panel_ref[n] = chosen[...]
+    panel_ref[n] = chosen[n]
+    for k in range(4, RING - 1):
+        spread_step(k)
     wait_all(own_copy)
     wait_all(panel_copy)
 
@@ -258,17 +331,18 @@
     vmem, anyspace = pl.BlockSpec(memory_space=pltpu.VMEM), pl.BlockSpec(memory_space=pl.ANY)
     dma = pltpu.SemaphoreType.DMA
     piece = jax.ShapeDtypeStruct((16, PIECE, 128), F32)
+    wider = jax.ShapeDtypeStruct((16, WIDER, 128), F32)
+    chunk = slab.shape[0] // RING // STREAMS
     return pl.pallas_call(
         gather_kernel,
-        out_shape=(piece, piece),
+        out_shape=(piece, wider, jax.ShapeDtypeStruct(slab.shape, BF16)),
         in_specs=[pl.BlockSpec(memory_space=pltpu.SMEM), vmem, vmem, anyspace, anyspace, anyspace],
-        out_specs=(vmem, vmem),
+        out_specs=(vmem, vmem, vmem),
         scratch_shapes=[
             pltpu.VMEM((6, funcs, layers, rows_y, depth), BF16),
             pltpu.VMEM((6, funcs, rows_y, depth), BF16),
             pltpu.VMEM((subs, layers, rows_y, depth), jnp.int32),
             pltpu.VMEM((subs, rows_y, depth), jnp.int32),
-            pltpu.VMEM((128, 128), BF16),
             pltpu.VMEM((6, layers, 5, rows_y, depth), F32),
             pltpu.VMEM((6, rows_y, depth), F32),
             pltpu.VMEM((layers, funcs * rows_y, depth), F32),
@@ -281,16 +355,21 @@
             pltpu.VMEM((16, PIECE, 128), F32),
             pltpu.VMEM((PIECE, 128), F32),
             pltpu.VMEM((16, PIECE, 128), F32),
-            pltpu.VMEM((PIECE, 128), F32),
+            pltpu.VMEM((16, WIDER, 128), F32),
+            pltpu.VMEM(slab.shape, BF16),
+            pltpu.VMEM((STREAMS, RING - 1, chunk, 128), BF16),
+            pltpu.VMEM((STREAMS, chunk, 128), BF16),
             dma((6,)), dma((2,)), dma((6,)), dma((6,)), dma, dma,
             dma((16,)), dma((16,)), dma((16,)), dma((16,)), dma((16,)), dma((16,)), dma((16,)), dma((16,)),
+            dma((STREAMS, RING - 1)), dma((STREAMS, RING - 1)), dma((STREAMS,)), dma((STREAMS,)),
+            dma((STREAMS, RING - 1)), dma((STREAMS, RING - 1)),
         ],
         compiler_params=pltpu.CompilerParams(collective_id=0, has_side_effects=True, vmem_limit_bytes=56 << 20),
         name="galerkin_gather",
     )(owner, table, ids, basis, mat, slab)
 
 
-def panel_kernel(owner_ref, panel_ref, own_ref, column_ref, rows_ref, slab_ref, out_ref, galerkin_ref, block, added_own, lower, parts, rows_bf):
+def panel_kernel(owner_ref, panel_ref, own_ref, column_ref, slab_ref, out_ref, galerkin_ref, block, added_own, lower, parts, rows_bf):
     w, n = lax.axis_index("wide"), lax.axis_index("narrow")
     owner = owner_ref[0]
     funcs = galerkin_ref.shape[1]
@@ -353,7 +432,8 @@
         y = lax.dot_general(x, parts[...], NT, preferred_element_type=F32)
         return y[:, 0:128] + (y[:, 128:256] + y[:, 256:384])
 
-    rows_bf[...] = solve(rows_ref[...]).astype(BF16)
+    rows = jnp.concatenate([panel_ref[q, 24:32, :] for q in range(16)], 0)
+    rows_bf[...] = solve(rows.astype(BF16)).astype(BF16)
     added_own[...] = jnp.zeros_like(added_own)
 
     @pl.when((w == n) & (n >= owner))
@@ -394,12 +474,12 @@
     store(done, height - done, solve(column_ref[rest, :]).astype(BF16), slab_ref[rest, :].astype(F32))
 
 
-def panel_step(owner, panel, own, column, rows, slab, funcs):
+def panel_step(owner, panel, own, column, slab, funcs):
     vmem = pl.BlockSpec(memory_space=pltpu.VMEM)
     return pl.pallas_call(
         panel_kernel,
         out_shape=(jax.ShapeDtypeStruct(slab.shape, BF16), jax.ShapeDtypeStruct((2, funcs, funcs), F32)),
-        in_specs=[pl.BlockSpec(memory_space=pltpu.SMEM)] + [vmem] * 5,
+        in_specs=[pl.BlockSpec(memory_space=pltpu.SMEM)] + [vmem] * 4,
         out_specs=(vmem, vmem),
         scratch_shapes=[
             pltpu.VMEM((128, 128), F32), pltpu.VMEM((128, 128), F32), pltpu.VMEM((128, 128), F32),
@@ -407,15 +487,12 @@
         ],
         compiler_params=pltpu.CompilerParams(vmem_limit_bytes=48 << 20),
         name="panel_step",
-    )(owner, panel, own, column, rows, slab)
+    )(owner, panel, own, column, slab)
 
 
 def on_device(coarse_basis, material_ids, lame_table, coarse_ids, coarse_slab, panel_owner):
-    w, n = lax.axis_index("wide"), lax.axis_index("narrow")
-    column = lax.psum(jnp.where(n == panel_owner[0], coarse_slab, 0).astype(BF16), "narrow")
-    rows = lax.psum(jnp.where(w == n, column[:128], 0).astype(BF16), "wide")
-    own, panel = gather(panel_owner, lame_table, coarse_ids, coarse_basis, material_ids, coarse_slab)
-    return panel_step(panel_owner, panel, own, column, rows, coarse_slab, coarse_basis.shape[1])
+    own, panel, column = gather(panel_owner, lame_table, coarse_ids, coarse_basis, material_ids, coarse_slab)
+    return panel_step(panel_owner, panel, own, column, coarse_slab, coarse_basis.shape[1])
 
 
 def solution(mesh):

time: 281 us -> 125 us (0.44)
  waiting for transfers between devices: 125 us -> 0 us
  blocking collectives: 52.9 us -> 0 us
  Pallas kernels: 83.2 us -> 120 us
  between operations: 14.7 us -> 1.31 us
    psum x1 -> x0, waiting for transfers between devices: 125 us -> none  [on_device(): lax.psum(jnp.where(n == panel_owner[0], coarse_slab, 0).astype(BF16), 'na...]
    psum x1 -> x0, blocking collectives: 52.9 us -> none  [on_device(): rows = lax.psum(jnp.where(w == n, column[:128], 0).astype(BF16), 'wide')]
    pallas_call x1, Pallas kernels: 66.8 us -> 103 us  [gather(): pl.pallas_call(gather_kernel, out_shape=(piece, wider, jax.ShapeDtypeStru...]
  transfers between devices with their start and end apart: 1 -> 0, of which waited for: 1 -> 0; matrix products, arithmetic and copies ran while one was open for 0% -> 0% of each run, Pallas kernels for 24% -> 0%
where the time goes in v2:
time: 125 us; the launch traced here: 124 us
  Pallas kernels  120 us (96%)
  local copies, waits for them, and re-layouts  3.28 us (3%)
  between operations  1.31 us (1%)
    pallas_call x1, Pallas kernels, gather(): pl.pallas_call(gather_kernel, out_shape=(piece, wider, jax.ShapeDtypeStru...  103 us
    pallas_call x1, Pallas kernels, panel_step(): pl.pallas_call(panel_kernel, out_shape=(jax.ShapeDtypeStruct(slab.shape,...  16.4 us
    unnamed x8, local copies, waits for them, and re-layouts  3.28 us

profile of v2, /device:TPU:32, one launch (start us, length us, event | category | flops | bytes accessed | tf_op | source)
XLA Modules:
  0.0 124.2 jit_solution(29994481941505518)
XLA Ops:
  1.3 0.0 copy-start
  1.3 103.1 %galerkin_gather.1 = (f32[16,24,128]{2,1,0:T(8,128)}, f32[16,32,128]{2,1,0:T(8,128)}, bf16[6144,128]{1,0:T(8,128)(2,1)}) custom-call(s32[1]{0:T(128)S(6)} %copy.8.owner_ref, bf16[2,16]{1,0:T(2,128)(2,1)} %table_ref.1, s32[2,96]{1,0:T(2,128)} %ids_ref.1, bf16[2,96,3,4,8,128]{5,4,3,2,1,0:T(8,128)(2,1)} %basis_ref.1, s32[2,4,8,128]{3,2,1,0:T(8,128)} %mat_ref.1, ...), custom_call_target="tpu_custom_call" | custom-call | tf_op jit(solution)/shard_map/galerkin_gather/pallas_call | solution.py:336
  104.4 0.0 copy-done
  104.4 0.0 copy-start.1
  104.5 1.4 %copy-done.1 = bf16[6144,128]{1,0:T(8,128)(2,1)S(1)} copy-done((bf16[6144,128]{1,0:T(8,128)(2,1)S(1)}, bf16[6144,128]{1,0:T(8,128)(2,1)}, u32[]{:S(2)}) %copy-start.1) | copy-done | bytes 1572888
  105.9 0.0 copy-start.2
  105.9 0.9 copy-done.2
  106.8 0.0 copy-start.3
  106.8 0.9 copy-done.3
  107.7 16.4 %panel_step.1 = (bf16[6144,128]{1,0:T(8,128)(2,1)}, f32[2,96,96]{2,1,0:T(8,128)}) custom-call(s32[1]{0:T(128)S(6)} %copy.8.owner_ref, f32[16,32,128]{2,1,0:T(8,128)S(1)} %copy-done.2, f32[16,24,128]{2,1,0:T(8,128)S(1)} %copy-done.3, bf16[6144,128]{1,0:T(8,128)(2,1)S(1)} %copy-done.1, bf16[6144,128]{1,0:T(8,128)(2,1)S(1)} %copy-done), custom_call_target="tpu_custom_call" | custom-call | tf_op jit(solution)/shard_map/panel_step/pallas_call | solution.py:479
Async XLA Ops:
  1.3 103.2 %copy-start = (bf16[6144,128]{1,0:T(8,128)(2,1)S(1)}, bf16[6144,128]{1,0:T(8,128)(2,1)}, u32[]{:S(2)}) copy-start(bf16[6144,128]{1,0:T(8,128)(2,1)} %slab_ref.3) | copy-start | bytes 4718596
  104.4 1.4 %copy-start.1 = (bf16[6144,128]{1,0:T(8,128)(2,1)S(1)}, bf16[6144,128]{1,0:T(8,128)(2,1)}, u32[]{:S(2)}) copy-start(bf16[6144,128]{1,0:T(8,128)(2,1)} %get-tuple-element.7.column_ref) | copy-start | bytes 4718596
  105.9 0.9 copy-start.2
  106.8 0.9 copy-start.3

commit v3 on v2

--- a/solution.py
+++ b/solution.py
@@ -13,8 +13,9 @@
 NN = (((1,), (0,)), ((), ()))
 PIECE = 24
 WIDER = 32
-STREAMS = 4
 RING = 8
+CHUNKS = 2
+STREAMS = ((-1, 4, 0), (-1, 4, 1), (1, 3, 0), (1, 3, 1))
 
 
 def exact_dot(a, b, dims):
@@ -41,7 +42,7 @@
     owner_ref, table_ref, ids_ref, basis_ref, mat_ref, slab_ref,
     own_ref, panel_ref, column_ref,
     tiles, halo, mats, mat_halo, coef, coef_halo, natural, left, right, first, acc, late,
-    pieces, landed, reduced, wide_in, chosen, slab, passing, swapped,
+    pieces, landed, reduced, wide_in, chosen, masked, passing, settled, swapped,
     load_sem, small_sem, halo_send, halo_recv, mat_send, mat_recv, rs_send, rs_recv,
     wide_send, wide_recv, own_send, own_recv, panel_send, panel_recv,
     ring_send, ring_recv, swap_send, swap_recv, spread_send, spread_recv,
@@ -66,13 +67,12 @@
 
     z, half = lax.div(n, 2), lax.rem(n, 2)
     piece_rows = column_ref.shape[0] // RING
-    chunk = piece_rows // STREAMS
-    way = lambda t: 1 if t % 2 == 0 else RING - 1
-    beside = lambda t: 2 * lax.rem(z + way(t), RING) + half
-    piece_at = lambda t, k: lax.rem(z + (RING - way(t)) * k, RING)
-
-    def chunk_rows(t, piece):
-        return pl.ds(pl.multiple_of(piece * piece_rows + t * chunk, chunk), chunk)
+    chunk = piece_rows // CHUNKS
+    ring = lambda shift: lax.rem(z + shift + RING, RING)
+    beside = lambda t: 2 * ring(STREAMS[t][0]) + half
+
+    def chunk_rows(c, piece):
+        return pl.ds(pl.multiple_of(piece * piece_rows + c * chunk, chunk), chunk)
 
     def ring_copy(t, k, source=None):
         return pltpu.make_async_remote_copy(
@@ -81,31 +81,41 @@
             device_id=(w, beside(t)), device_id_type=MESH)
 
     def ring_start(t):
-        ring_copy(t, 0, slab.at[chunk_rows(t, piece_at(t, 1))]).start()
-
-    def ring_land(t, k):
+        way, steps, c = STREAMS[t]
+        ring_copy(t, 0, masked.at[chunk_rows(c, ring(way * steps))]).start()
+
+    def ring_step(t, k, last):
+        way, steps, c = STREAMS[t]
         ring_copy(t, k, passing.at[t, k]).wait()
-        passing[t, k] += slab[chunk_rows(t, piece_at(t, k + 2)), :]
-
-    def swap_copy(t):
-        return pltpu.make_async_remote_copy(
-            src_ref=passing.at[t, RING - 2], dst_ref=swapped.at[t], send_sem=swap_send.at[t], recv_sem=swap_recv.at[t],
+        if not last:
+            passing[t, k] += masked[chunk_rows(c, ring(way * (steps - 1 - k))), :]
+            ring_copy(t, k + 1, passing.at[t, k]).start()
+
+    def swap_copy(c):
+        return pltpu.make_async_remote_copy(
+            src_ref=settled.at[c], dst_ref=swapped.at[c], send_sem=swap_send.at[c], recv_sem=swap_recv.at[c],
             device_id=(w, n + 1 - 2 * half), device_id_type=MESH)
 
+    def swap_start(c):
+        settled[c] = passing[c, 3] + passing[CHUNKS + c, 2] + masked[chunk_rows(c, z), :]
+        swap_copy(c).start()
+
     def spread_copy(t, k):
-        part = column_ref.at[chunk_rows(t, piece_at(t, k))]
+        way, steps, c = STREAMS[t]
+        part = column_ref.at[chunk_rows(c, ring(-way * k))]
         return pltpu.make_async_remote_copy(
             src_ref=part, dst_ref=part, send_sem=spread_send.at[t, k], recv_sem=spread_recv.at[t, k],
             device_id=(w, beside(t)), device_id_type=MESH)
 
     def spread_step(k):
-        for t in range(STREAMS):
-            spread_copy(t, k).wait()
-            if k + 1 < RING - 1:
+        for t, (way, steps, c) in enumerate(STREAMS):
+            if k < steps:
+                spread_copy(t, k).wait()
+            if k + 1 < steps:
                 spread_copy(t, k + 1).start()
 
     mat_copy = pltpu.make_async_copy(mat_ref, mats, small_sem.at[0])
-    slab_copy = pltpu.make_async_copy(slab_ref, slab, small_sem.at[1])
+    slab_copy = pltpu.make_async_copy(slab_ref, masked, small_sem.at[1])
     mat_halo_copy = pltpu.make_async_remote_copy(
         src_ref=mat_ref.at[:, layers - 1], dst_ref=mat_halo, send_sem=mat_send, recv_sem=mat_recv,
         device_id=(w, group(1)), device_id_type=MESH)
@@ -128,7 +138,7 @@
 
     def mask(q, carry):
         part = pl.ds(pl.multiple_of(q * piece_rows, piece_rows), piece_rows)
-        slab[part, :] = slab[part, :] * mine
+        masked[part, :] = masked[part, :] * mine
         return carry
 
     lax.fori_loop(0, RING, mask, 0)
@@ -137,7 +147,7 @@
     mat_halo_copy.start()
     for sc in range(6):
         halo_copy(sc).start()
-    for t in range(STREAMS):
+    for t in range(len(STREAMS)):
         ring_start(t)
 
     acc[...] = jnp.zeros_like(acc)
@@ -227,18 +237,33 @@
                 right[0:funcs, lanes] = hi
                 right[128:128 + funcs, lanes] = lo
             acc[s] += lax.dot_general(left[...], right[...], NT, preferred_element_type=F32)
-            ring_land(i, sc)
-            ring_copy(i, sc + 1).start()
+
+        @pl.when((sc >= 1) & (sc <= 2))
+        def _():
+            for t in range(len(STREAMS)):
+                ring_step(t, sc - 1, False)
+
+        @pl.when(sc == 3)
+        def _():
+            for t in range(CHUNKS):
+                ring_step(t, 2, False)
+            for t in range(CHUNKS, 2 * CHUNKS):
+                ring_step(t, 2, True)
+
+        @pl.when(sc == 4)
+        def _():
+            for c in range(CHUNKS):
+                ring_step(c, 3, True)
+                swap_start(c)
+
         return carry
 
     lax.fori_loop(0, 6, interior, 0)
-    for t in range(STREAMS):
-        ring_land(t, RING - 2)
-        swap_copy(t).start()
-    for t in range(STREAMS):
-        swap_copy(t).wait()
-        column_ref[chunk_rows(t, z), :] = passing[t, RING - 2] + swapped[t]
-        spread_copy(t, 0).start()
+    for c in range(CHUNKS):
+        swap_copy(c).wait()
+        column_ref[chunk_rows(c, z), :] = settled[c] + swapped[c]
+        for t in (c, CHUNKS + c):
+            spread_copy(t, 0).start()
 
     def boundary(sc, carry):
         s = lax.div(sc, 3)
@@ -255,11 +280,11 @@
         late[s, funcs:2 * funcs] += lax.dot_general(first[sc], right[...], NT, preferred_element_type=F32)
         return carry
 
-    lax.fori_loop(0, 3, boundary, 0)
+    lax.fori_loop(0, 4, boundary, 0)
     spread_step(0)
-    lax.fori_loop(3, 6, boundary, 0)
-
-    head = slab[0:128, :].astype(F32)
+    lax.fori_loop(4, 6, boundary, 0)
+
+    head = masked[0:128, :].astype(F32)
     for q in range(16):
         pieces[q, 16:24, :] = head[8 * q:8 * (q + 1), :]
     for s in range(2):
@@ -300,7 +325,6 @@
     start_all(rs_copy)
     landed[n] = pieces[n]
     spread_step(1)
-    spread_step(2)
     wait_all(rs_copy)
     total = landed[0]
     for q in range(1, 16):
@@ -309,21 +333,20 @@
     reduced[12:14, :] = jnp.full((2, 128), -1.0, F32)
     reduced[12:14, 0:funcs] = ids_ref[...].astype(F32)
     start_all(wide_copy)
-    start_all(own_copy)
     own_ref[n] = reduced[...]
     wide_in[w] = reduced[...]
-    spread_step(3)
+    spread_step(2)
     wait_all(wide_copy)
     of_owner = wide_in[owner_ref[0]]
     for q in range(16):
         chosen[q, 0:24, :] = of_owner
         chosen[q, 24:32, :] = wide_in[q, 16:24, :]
     start_all(panel_copy)
+    start_all(own_copy)
     panel_ref[n] = chosen[n]
-    for k in range(4, RING - 1):
-        spread_step(k)
+    spread_step(3)
+    wait_all(panel_copy)
     wait_all(own_copy)
-    wait_all(panel_copy)
 
 
 def gather(owner, table, ids, basis, mat, slab):
@@ -332,7 +355,8 @@
     dma = pltpu.SemaphoreType.DMA
     piece = jax.ShapeDtypeStruct((16, PIECE, 128), F32)
     wider = jax.ShapeDtypeStruct((16, WIDER, 128), F32)
-    chunk = slab.shape[0] // RING // STREAMS
+    chunk = slab.shape[0] // RING // CHUNKS
+    streams = len(STREAMS)
     return pl.pallas_call(
         gather_kernel,
         out_shape=(piece, wider, jax.ShapeDtypeStruct(slab.shape, BF16)),
@@ -357,21 +381,28 @@
             pltpu.VMEM((16, PIECE, 128), F32),
             pltpu.VMEM((16, WIDER, 128), F32),
             pltpu.VMEM(slab.shape, BF16),
-            pltpu.VMEM((STREAMS, RING - 1, chunk, 128), BF16),
-            pltpu.VMEM((STREAMS, chunk, 128), BF16),
+            pltpu.VMEM((streams, 4, chunk, 128), BF16),
+            pltpu.VMEM((CHUNKS, chunk, 128), BF16),
+            pltpu.VMEM((CHUNKS, chunk, 128), BF16),
             dma((6,)), dma((2,)), dma((6,)), dma((6,)), dma, dma,
             dma((16,)), dma((16,)), dma((16,)), dma((16,)), dma((16,)), dma((16,)), dma((16,)), dma((16,)),
-            dma((STREAMS, RING - 1)), dma((STREAMS, RING - 1)), dma((STREAMS,)), dma((STREAMS,)),
-            dma((STREAMS, RING - 1)), dma((STREAMS, RING - 1)),
+            dma((streams, 4)), dma((streams, 4)), dma((CHUNKS,)), dma((CHUNKS,)), dma((streams, 4)), dma((streams, 4)),
         ],
-        compiler_params=pltpu.CompilerParams(collective_id=0, has_side_effects=True, vmem_limit_bytes=56 << 20),
+        compiler_params=pltpu.CompilerParams(collective_id=0, has_side_effects=True, vmem_limit_bytes=63 << 20),
         name="galerkin_gather",
     )(owner, table, ids, basis, mat, slab)
 
 
-def panel_kernel(owner_ref, panel_ref, own_ref, column_ref, slab_ref, out_ref, galerkin_ref, block, added_own, lower, parts, rows_bf):
+def panel_kernel(
+    owner_ref, panel_hbm, own_hbm, column_hbm, slab_hbm, out_ref, galerkin_ref,
+    panel_ref, own_ref, column_ref, slab_ref, block, added_own, lower, parts, rows_bf, load_sem,
+):
     w, n = lax.axis_index("wide"), lax.axis_index("narrow")
     owner = owner_ref[0]
+    pairs = ((panel_hbm, panel_ref), (own_hbm, own_ref), (column_hbm, column_ref), (slab_hbm, slab_ref))
+    loads = [pltpu.make_async_copy(src, dst, load_sem.at[q]) for q, (src, dst) in enumerate(pairs)]
+    for copy in loads:
+        copy.start()
     funcs = galerkin_ref.shape[1]
     height, tile = out_ref.shape[0], 512
 
@@ -390,10 +421,7 @@
         return total
 
     block[...] = jnp.zeros_like(block)
-    for s in range(2):
-        for z in range(8):
-            galerkin_ref[s, 12 * z:12 * (z + 1), :] = own_ref[2 * z + s, 0:12, 0:funcs]
-
+    loads[0].wait()
     diagonal = added_of(panel_ref) + jnp.concatenate([panel_ref[q, 16:24, :] for q in range(16)], 0)
     diagonal = 0.5 * (diagonal + diagonal.T)
     sub = lax.broadcasted_iota(jnp.int32, (8, 128), 0)
@@ -432,6 +460,12 @@
         y = lax.dot_general(x, parts[...], NT, preferred_element_type=F32)
         return y[:, 0:128] + (y[:, 128:256] + y[:, 256:384])
 
+    loads[1].wait()
+    for s in range(2):
+        for z in range(8):
+            galerkin_ref[s, 12 * z:12 * (z + 1), :] = own_ref[2 * z + s, 0:12, 0:funcs]
+    loads[2].wait()
+    loads[3].wait()
     rows = jnp.concatenate([panel_ref[q, 24:32, :] for q in range(16)], 0)
     rows_bf[...] = solve(rows.astype(BF16)).astype(BF16)
     added_own[...] = jnp.zeros_like(added_own)
@@ -479,13 +513,15 @@
     return pl.pallas_call(
         panel_kernel,
         out_shape=(jax.ShapeDtypeStruct(slab.shape, BF16), jax.ShapeDtypeStruct((2, funcs, funcs), F32)),
-        in_specs=[pl.BlockSpec(memory_space=pltpu.SMEM)] + [vmem] * 4,
+        in_specs=[pl.BlockSpec(memory_space=pltpu.SMEM)] + [pl.BlockSpec(memory_space=pl.ANY)] * 4,
         out_specs=(vmem, vmem),
         scratch_shapes=[
+            pltpu.VMEM(panel.shape, F32), pltpu.VMEM(own.shape, F32), pltpu.VMEM(slab.shape, BF16), pltpu.VMEM(slab.shape, BF16),
             pltpu.VMEM((128, 128), F32), pltpu.VMEM((128, 128), F32), pltpu.VMEM((128, 128), F32),
             pltpu.VMEM((384, 128), BF16), pltpu.VMEM((128, 128), BF16),
+            pltpu.SemaphoreType.DMA((4,)),
         ],
-        compiler_params=pltpu.CompilerParams(vmem_limit_bytes=48 << 20),
+        compiler_params=pltpu.CompilerParams(vmem_limit_bytes=63 << 20),
         name="panel_step",
     )(owner, panel, own, column, slab)
 

time: 125 us -> 119 us (0.952)
  Pallas kernels: 120 us -> 116 us
  local copies, waits for them, and re-layouts: 3.28 us -> 0 us
    pallas_call x1, Pallas kernels: 103 us -> 98.8 us  [gather(): pl.pallas_call(gather_kernel, out_shape=(piece, wider, jax.ShapeDtypeStru...]
    unnamed x8 -> x0, local copies, waits for them, and re-layouts: 3.28 us -> none
where the time goes in v3:
time: 119 us; the launch traced here: 117 us
  Pallas kernels  116 us (97%)
  between operations  1.29 us (1%)
    pallas_call x1, Pallas kernels, gather(): pl.pallas_call(gather_kernel, out_shape=(piece, wider, jax.ShapeDtypeStru...  98.8 us
    pallas_call x1, Pallas kernels, panel_step(): pl.pallas_call(panel_kernel, out_shape=(jax.ShapeDtypeStruct(slab.shape,...  17.4 us

profile of v3, /device:TPU:32, one launch (start us, length us, event | category | flops | bytes accessed | tf_op | source)
XLA Modules:
  0.0 117.4 jit_solution(2442712691687907611)
XLA Ops:
  1.3 98.8 %galerkin_gather.1 = (f32[16,24,128]{2,1,0:T(8,128)}, f32[16,32,128]{2,1,0:T(8,128)}, bf16[6144,128]{1,0:T(8,128)(2,1)}) custom-call(s32[1]{0:T(128)S(6)} %copy.8.owner_ref, bf16[2,16]{1,0:T(2,128)(2,1)} %table_ref.1, s32[2,96]{1,0:T(2,128)} %ids_ref.1, bf16[2,96,3,4,8,128]{5,4,3,2,1,0:T(8,128)(2,1)} %basis_ref.1, s32[2,4,8,128]{3,2,1,0:T(8,128)} %mat_ref.1, ...), custom_call_target="tpu_custom_call" | custom-call | tf_op jit(solution)/shard_map/galerkin_gather/pallas_call | solution.py:360
  100.0 17.4 %panel_step.1 = (bf16[6144,128]{1,0:T(8,128)(2,1)}, f32[2,96,96]{2,1,0:T(8,128)}) custom-call(s32[1]{0:T(128)S(6)} %copy.8.owner_ref, f32[16,32,128]{2,1,0:T(8,128)} %get-tuple-element.5.panel_hbm, f32[16,24,128]{2,1,0:T(8,128)} %get-tuple-element.6.own_hbm, bf16[6144,128]{1,0:T(8,128)(2,1)} %get-tuple-element.7.column_hbm, bf16[6144,128]{1,0:T(8,128)(2,1)} %slab_hbm.1), custom_call_target="tpu_custom_call" | custom-call | tf_op jit(solution)/shard_map/panel_step/pallas_call | solution.py:513

commit v4 on v3

--- a/solution.py
+++ b/solution.py
@@ -15,7 +15,8 @@
 WIDER = 32
 RING = 8
 CHUNKS = 2
-STREAMS = ((-1, 4, 0), (-1, 4, 1), (1, 3, 0), (1, 3, 1))
+SUMS = ((-1, 6, 0), (-1, 6, 1), (1, 1, 0), (1, 1, 1))
+SPREAD = ((-1, 4, 0), (-1, 4, 1), (1, 3, 0), (1, 3, 1))
 
 
 def exact_dot(a, b, dims):
@@ -69,7 +70,7 @@
     piece_rows = column_ref.shape[0] // RING
     chunk = piece_rows // CHUNKS
     ring = lambda shift: lax.rem(z + shift + RING, RING)
-    beside = lambda t: 2 * ring(STREAMS[t][0]) + half
+    beside = lambda way: 2 * ring(way) + half
 
     def chunk_rows(c, piece):
         return pl.ds(pl.multiple_of(piece * piece_rows + c * chunk, chunk), chunk)
@@ -78,14 +79,14 @@
         return pltpu.make_async_remote_copy(
             src_ref=passing.at[t, k - 1] if source is None else source, dst_ref=passing.at[t, k],
             send_sem=ring_send.at[t, k], recv_sem=ring_recv.at[t, k],
-            device_id=(w, beside(t)), device_id_type=MESH)
+            device_id=(w, beside(SUMS[t][0])), device_id_type=MESH)
 
     def ring_start(t):
-        way, steps, c = STREAMS[t]
+        way, steps, c = SUMS[t]
         ring_copy(t, 0, masked.at[chunk_rows(c, ring(way * steps))]).start()
 
     def ring_step(t, k, last):
-        way, steps, c = STREAMS[t]
+        way, steps, c = SUMS[t]
         ring_copy(t, k, passing.at[t, k]).wait()
         if not last:
             passing[t, k] += masked[chunk_rows(c, ring(way * (steps - 1 - k))), :]
@@ -97,18 +98,18 @@
             device_id=(w, n + 1 - 2 * half), device_id_type=MESH)
 
     def swap_start(c):
-        settled[c] = passing[c, 3] + passing[CHUNKS + c, 2] + masked[chunk_rows(c, z), :]
+        settled[c] = passing[c, SUMS[0][1] - 1] + passing[CHUNKS + c, SUMS[2][1] - 1] + masked[chunk_rows(c, z), :]
         swap_copy(c).start()
 
     def spread_copy(t, k):
-        way, steps, c = STREAMS[t]
+        way, steps, c = SPREAD[t]
         part = column_ref.at[chunk_rows(c, ring(-way * k))]
         return pltpu.make_async_remote_copy(
             src_ref=part, dst_ref=part, send_sem=spread_send.at[t, k], recv_sem=spread_recv.at[t, k],
-            device_id=(w, beside(t)), device_id_type=MESH)
+            device_id=(w, beside(way)), device_id_type=MESH)
 
     def spread_step(k):
-        for t, (way, steps, c) in enumerate(STREAMS):
+        for t, (way, steps, c) in enumerate(SPREAD):
             if k < steps:
                 spread_copy(t, k).wait()
             if k + 1 < steps:
@@ -145,10 +146,10 @@
     pl.semaphore_wait(barrier, 2 * (count - 1))
 
     mat_halo_copy.start()
-    for sc in range(6):
+    for t in range(len(SUMS)):
+        ring_start(t)
+    for sc in range(2):
         halo_copy(sc).start()
-    for t in range(len(STREAMS)):
-        ring_start(t)
 
     acc[...] = jnp.zeros_like(acc)
     late[...] = jnp.zeros_like(late)
@@ -237,37 +238,23 @@
                 right[0:funcs, lanes] = hi
                 right[128:128 + funcs, lanes] = lo
             acc[s] += lax.dot_general(left[...], right[...], NT, preferred_element_type=F32)
-
-        @pl.when((sc >= 1) & (sc <= 2))
+        halo_copy(sc).wait_send()
+
+        @pl.when(sc < 4)
         def _():
-            for t in range(len(STREAMS)):
-                ring_step(t, sc - 1, False)
-
-        @pl.when(sc == 3)
+            halo_copy(sc + 2).start()
+
+        @pl.when(sc >= 1)
         def _():
             for t in range(CHUNKS):
-                ring_step(t, 2, False)
-            for t in range(CHUNKS, 2 * CHUNKS):
-                ring_step(t, 2, True)
-
-        @pl.when(sc == 4)
-        def _():
-            for c in range(CHUNKS):
-                ring_step(c, 3, True)
-                swap_start(c)
+                ring_step(t, sc - 1, False)
 
         return carry
 
     lax.fori_loop(0, 6, interior, 0)
-    for c in range(CHUNKS):
-        swap_copy(c).wait()
-        column_ref[chunk_rows(c, z), :] = settled[c] + swapped[c]
-        for t in (c, CHUNKS + c):
-            spread_copy(t, 0).start()
-
     def boundary(sc, carry):
         s = lax.div(sc, 3)
-        halo_copy(sc).wait()
+        halo_copy(sc).wait_recv()
         natural[0] = halo[sc].astype(F32).reshape(funcs * rows_y, 128)
         for y in range(rows_y):
             h = natural[0, pl.ds(y, funcs, stride=rows_y), :]
@@ -280,9 +267,7 @@
         late[s, funcs:2 * funcs] += lax.dot_general(first[sc], right[...], NT, preferred_element_type=F32)
         return carry
 
-    lax.fori_loop(0, 4, boundary, 0)
-    spread_step(0)
-    lax.fori_loop(4, 6, boundary, 0)
+    lax.fori_loop(0, 6, boundary, 0)
 
     head = masked[0:128, :].astype(F32)
     for q in range(16):
@@ -324,7 +309,10 @@
 
     start_all(rs_copy)
     landed[n] = pieces[n]
-    spread_step(1)
+    for c in range(CHUNKS):
+        ring_step(c, SUMS[0][1] - 1, True)
+        ring_step(CHUNKS + c, 0, True)
+        swap_start(c)
     wait_all(rs_copy)
     total = landed[0]
     for q in range(1, 16):
@@ -333,18 +321,23 @@
     reduced[12:14, :] = jnp.full((2, 128), -1.0, F32)
     reduced[12:14, 0:funcs] = ids_ref[...].astype(F32)
     start_all(wide_copy)
+    start_all(own_copy)
     own_ref[n] = reduced[...]
     wide_in[w] = reduced[...]
-    spread_step(2)
+    for c in range(CHUNKS):
+        swap_copy(c).wait()
+        column_ref[chunk_rows(c, z), :] = settled[c] + swapped[c]
+        for t in (c, CHUNKS + c):
+            spread_copy(t, 0).start()
     wait_all(wide_copy)
     of_owner = wide_in[owner_ref[0]]
     for q in range(16):
         chosen[q, 0:24, :] = of_owner
         chosen[q, 24:32, :] = wide_in[q, 16:24, :]
     start_all(panel_copy)
-    start_all(own_copy)
     panel_ref[n] = chosen[n]
-    spread_step(3)
+    for k in range(4):
+        spread_step(k)
     wait_all(panel_copy)
     wait_all(own_copy)
 
@@ -356,7 +349,7 @@
     piece = jax.ShapeDtypeStruct((16, PIECE, 128), F32)
     wider = jax.ShapeDtypeStruct((16, WIDER, 128), F32)
     chunk = slab.shape[0] // RING // CHUNKS
-    streams = len(STREAMS)
+    streams, longest = len(SUMS), max(steps for _, steps, _ in SUMS)
     return pl.pallas_call(
         gather_kernel,
         out_shape=(piece, wider, jax.ShapeDtypeStruct(slab.shape, BF16)),
@@ -381,12 +374,12 @@
             pltpu.VMEM((16, PIECE, 128), F32),
             pltpu.VMEM((16, WIDER, 128), F32),
             pltpu.VMEM(slab.shape, BF16),
-            pltpu.VMEM((streams, 4, chunk, 128), BF16),
+            pltpu.VMEM((streams, longest, chunk, 128), BF16),
             pltpu.VMEM((CHUNKS, chunk, 128), BF16),
             pltpu.VMEM((CHUNKS, chunk, 128), BF16),
             dma((6,)), dma((2,)), dma((6,)), dma((6,)), dma, dma,
             dma((16,)), dma((16,)), dma((16,)), dma((16,)), dma((16,)), dma((16,)), dma((16,)), dma((16,)),
-            dma((streams, 4)), dma((streams, 4)), dma((CHUNKS,)), dma((CHUNKS,)), dma((streams, 4)), dma((streams, 4)),
+            dma((streams, longest)), dma((streams, longest)), dma((CHUNKS,)), dma((CHUNKS,)), dma((streams, 4)), dma((streams, 4)),
         ],
         compiler_params=pltpu.CompilerParams(collective_id=0, has_side_effects=True, vmem_limit_bytes=63 << 20),
         name="galerkin_gather",

time: 119 us -> 103 us (0.87)
  Pallas kernels: 116 us -> 100 us
    pallas_call x1, Pallas kernels: 98.8 us -> 82.9 us  [gather(): pl.pallas_call(gather_kernel, out_shape=(piece, wider, jax.ShapeDtypeStru...]
where the time goes in v4:
time: 103 us; the launch traced here: 102 us
  Pallas kernels  100 us (97%)
  between operations  1.29 us (1%)
    pallas_call x1, Pallas kernels, gather(): pl.pallas_call(gather_kernel, out_shape=(piece, wider, jax.ShapeDtypeStru...  82.9 us
    pallas_call x1, Pallas kernels, panel_step(): pl.pallas_call(panel_kernel, out_shape=(jax.ShapeDtypeStruct(slab.shape,...  17.5 us

profile of v4, /device:TPU:32, one launch (start us, length us, event | category | flops | bytes accessed | tf_op | source)
XLA Modules:
  0.0 101.7 jit_solution(14598996069381845812)
XLA Ops:
  1.3 82.9 %galerkin_gather.1 = (f32[16,24,128]{2,1,0:T(8,128)}, f32[16,32,128]{2,1,0:T(8,128)}, bf16[6144,128]{1,0:T(8,128)(2,1)}) custom-call(s32[1]{0:T(128)S(6)} %copy.8.owner_ref, bf16[2,16]{1,0:T(2,128)(2,1)} %table_ref.1, s32[2,96]{1,0:T(2,128)} %ids_ref.1, bf16[2,96,3,4,8,128]{5,4,3,2,1,0:T(8,128)(2,1)} %basis_ref.1, s32[2,4,8,128]{3,2,1,0:T(8,128)} %mat_ref.1, ...), custom_call_target="tpu_custom_call" | custom-call | tf_op jit(solution)/shard_map/galerkin_gather/pallas_call | solution.py:353
  84.2 17.5 %panel_step.1 = (bf16[6144,128]{1,0:T(8,128)(2,1)}, f32[2,96,96]{2,1,0:T(8,128)}) custom-call(s32[1]{0:T(128)S(6)} %copy.8.owner_ref, f32[16,32,128]{2,1,0:T(8,128)} %get-tuple-element.5.panel_hbm, f32[16,24,128]{2,1,0:T(8,128)} %get-tuple-element.6.own_hbm, bf16[6144,128]{1,0:T(8,128)(2,1)} %get-tuple-element.7.column_hbm, bf16[6144,128]{1,0:T(8,128)(2,1)} %slab_hbm.1), custom_call_target="tpu_custom_call" | custom-call | tf_op jit(solution)/shard_map/panel_step/pallas_call | solution.py:506

commit v5 on v4

--- a/solution.py
+++ b/solution.py
@@ -14,6 +14,7 @@
 PIECE = 24
 WIDER = 32
 RING = 8
+TILES = 8
 CHUNKS = 2
 SUMS = ((-1, 6, 0), (-1, 6, 1), (1, 1, 0), (1, 1, 1))
 SPREAD = ((-1, 4, 0), (-1, 4, 1), (1, 3, 0), (1, 3, 1))
@@ -39,11 +40,27 @@
     return jnp.where(index == size - 1, 0.0, pltpu.roll(x, size - 1, axis))
 
 
+def added_of(pieces_ref, block):
+    total = jnp.zeros((128, 128), F32)
+    index = lax.broadcasted_iota(jnp.int32, (128, 128), 0).astype(F32)
+    for s in range(2):
+        place = jnp.where(index == pieces_ref[0, 12 + s:13 + s, :], 1.0, 0.0)
+        for part in range(RING):
+            block[12 * part:12 * (part + 1), :] = pieces_ref[2 * part + s, 0:12, :]
+        total = total + exact_dot(exact_dot(place, block[...], NN), place, NT)
+    return total
+
+
+def solve(x, parts):
+    y = lax.dot_general(x, parts, NT, preferred_element_type=F32)
+    return y[:, 0:128] + (y[:, 128:256] + y[:, 256:384])
+
+
 def gather_kernel(
     owner_ref, table_ref, ids_ref, basis_ref, mat_ref, slab_ref,
-    own_ref, panel_ref, column_ref,
+    own_ref, column_ref, parts_ref, lower_ref, rows_ref,
     tiles, halo, mats, mat_halo, coef, coef_halo, natural, left, right, first, acc, late,
-    pieces, landed, reduced, wide_in, chosen, masked, passing, settled, swapped,
+    pieces, landed, reduced, wide_in, chosen, panel_ref, block, masked, passing, settled, swapped,
     load_sem, small_sem, halo_send, halo_recv, mat_send, mat_recv, rs_send, rs_recv,
     wide_send, wide_recv, own_send, own_recv, panel_send, panel_recv,
     ring_send, ring_recv, swap_send, swap_recv, spread_send, spread_recv,
@@ -336,92 +353,20 @@
         chosen[q, 24:32, :] = wide_in[q, 16:24, :]
     start_all(panel_copy)
     panel_ref[n] = chosen[n]
-    for k in range(4):
-        spread_step(k)
+    block[...] = jnp.zeros_like(block)
+    spread_step(0)
+    spread_step(1)
     wait_all(panel_copy)
-    wait_all(own_copy)
-
-
-def gather(owner, table, ids, basis, mat, slab):
-    subs, funcs, comps, layers, rows_y, depth = basis.shape
-    vmem, anyspace = pl.BlockSpec(memory_space=pltpu.VMEM), pl.BlockSpec(memory_space=pl.ANY)
-    dma = pltpu.SemaphoreType.DMA
-    piece = jax.ShapeDtypeStruct((16, PIECE, 128), F32)
-    wider = jax.ShapeDtypeStruct((16, WIDER, 128), F32)
-    chunk = slab.shape[0] // RING // CHUNKS
-    streams, longest = len(SUMS), max(steps for _, steps, _ in SUMS)
-    return pl.pallas_call(
-        gather_kernel,
-        out_shape=(piece, wider, jax.ShapeDtypeStruct(slab.shape, BF16)),
-        in_specs=[pl.BlockSpec(memory_space=pltpu.SMEM), vmem, vmem, anyspace, anyspace, anyspace],
-        out_specs=(vmem, vmem, vmem),
-        scratch_shapes=[
-            pltpu.VMEM((6, funcs, layers, rows_y, depth), BF16),
-            pltpu.VMEM((6, funcs, rows_y, depth), BF16),
-            pltpu.VMEM((subs, layers, rows_y, depth), jnp.int32),
-            pltpu.VMEM((subs, rows_y, depth), jnp.int32),
-            pltpu.VMEM((6, layers, 5, rows_y, depth), F32),
-            pltpu.VMEM((6, rows_y, depth), F32),
-            pltpu.VMEM((layers, funcs * rows_y, depth), F32),
-            pltpu.VMEM((funcs, rows_y * depth), BF16),
-            pltpu.VMEM((256, rows_y * depth), BF16),
-            pltpu.VMEM((6, funcs, rows_y * depth), BF16),
-            pltpu.VMEM((subs, funcs, 256), F32),
-            pltpu.VMEM((subs, 2 * funcs, 256), F32),
-            pltpu.VMEM((16, PIECE, 128), F32),
-            pltpu.VMEM((16, PIECE, 128), F32),
-            pltpu.VMEM((PIECE, 128), F32),
-            pltpu.VMEM((16, PIECE, 128), F32),
-            pltpu.VMEM((16, WIDER, 128), F32),
-            pltpu.VMEM(slab.shape, BF16),
-            pltpu.VMEM((streams, longest, chunk, 128), BF16),
-            pltpu.VMEM((CHUNKS, chunk, 128), BF16),
-            pltpu.VMEM((CHUNKS, chunk, 128), BF16),
-            dma((6,)), dma((2,)), dma((6,)), dma((6,)), dma, dma,
-            dma((16,)), dma((16,)), dma((16,)), dma((16,)), dma((16,)), dma((16,)), dma((16,)), dma((16,)),
-            dma((streams, longest)), dma((streams, longest)), dma((CHUNKS,)), dma((CHUNKS,)), dma((streams, 4)), dma((streams, 4)),
-        ],
-        compiler_params=pltpu.CompilerParams(collective_id=0, has_side_effects=True, vmem_limit_bytes=63 << 20),
-        name="galerkin_gather",
-    )(owner, table, ids, basis, mat, slab)
-
-
-def panel_kernel(
-    owner_ref, panel_hbm, own_hbm, column_hbm, slab_hbm, out_ref, galerkin_ref,
-    panel_ref, own_ref, column_ref, slab_ref, block, added_own, lower, parts, rows_bf, load_sem,
-):
-    w, n = lax.axis_index("wide"), lax.axis_index("narrow")
-    owner = owner_ref[0]
-    pairs = ((panel_hbm, panel_ref), (own_hbm, own_ref), (column_hbm, column_ref), (slab_hbm, slab_ref))
-    loads = [pltpu.make_async_copy(src, dst, load_sem.at[q]) for q, (src, dst) in enumerate(pairs)]
-    for copy in loads:
-        copy.start()
-    funcs = galerkin_ref.shape[1]
-    height, tile = out_ref.shape[0], 512
-
-    def slots(pieces_ref, s):
-        ids = pieces_ref[0, 12 + s:13 + s, :]
-        index = lax.broadcasted_iota(jnp.int32, (128, 128), 0).astype(F32)
-        return jnp.where(index == ids, 1.0, 0.0)
-
-    def added_of(pieces_ref):
-        total = jnp.zeros((128, 128), F32)
-        for s in range(2):
-            place = slots(pieces_ref, s)
-            for z in range(8):
-                block[12 * z:12 * (z + 1), :] = pieces_ref[2 * z + s, 0:12, :]
-            total = total + exact_dot(exact_dot(place, block[...], NN), place, NT)
-        return total
-
-    block[...] = jnp.zeros_like(block)
-    loads[0].wait()
-    diagonal = added_of(panel_ref) + jnp.concatenate([panel_ref[q, 16:24, :] for q in range(16)], 0)
+
+    diagonal = added_of(panel_ref, block) + jnp.concatenate([panel_ref[q, 16:24, :] for q in range(16)], 0)
     diagonal = 0.5 * (diagonal + diagonal.T)
     sub = lax.broadcasted_iota(jnp.int32, (8, 128), 0)
     lane = lax.broadcasted_iota(jnp.int32, (8, 128), 1)
     a = [diagonal[8 * b:8 * (b + 1)] for b in range(16)]
     m = [jnp.where(lane == sub + 8 * b, 1.0, 0.0) for b in range(16)]
     for j in range(128):
+        if j == 64:
+            spread_step(2)
         b0, r = divmod(j, 8)
         row_a, row_m = a[b0][r:r + 1], m[b0][r:r + 1]
         inverse = 1.0 / row_a[:, j:j + 1]
@@ -441,87 +386,160 @@
         scale = lax.rsqrt(d)
         upper.append(jnp.where(lane >= sub + 8 * b, a[b] * scale, 0.0))
         m[b] = m[b] * scale
-    lower[...] = jnp.concatenate(upper, 0).T
+    lower_ref[...] = jnp.concatenate(upper, 0).T
     inverse = jnp.concatenate(m, 0)
     hi, rest = split2(inverse)
     mid, low = split2(inverse - hi.astype(F32))
-    parts[0:128] = hi
-    parts[128:256] = mid
-    parts[256:384] = low
-
-    def solve(x):
-        y = lax.dot_general(x, parts[...], NT, preferred_element_type=F32)
-        return y[:, 0:128] + (y[:, 128:256] + y[:, 256:384])
-
-    loads[1].wait()
+    parts_ref[0:128] = hi
+    parts_ref[128:256] = mid
+    parts_ref[256:384] = low
+
+    rows = jnp.concatenate([panel_ref[q, 24:32, :] for q in range(16)], 0)
+    rows_ref[...] = solve(rows.astype(BF16), parts_ref[...]).astype(BF16)
+    spread_step(3)
+    wait_all(own_copy)
+
+
+def gather(owner, table, ids, basis, mat, slab):
+    subs, funcs, comps, layers, rows_y, depth = basis.shape
+    vmem, anyspace = pl.BlockSpec(memory_space=pltpu.VMEM), pl.BlockSpec(memory_space=pl.ANY)
+    dma = pltpu.SemaphoreType.DMA
+    piece = jax.ShapeDtypeStruct((16, PIECE, 128), F32)
+    chunk = slab.shape[0] // RING // CHUNKS
+    streams, longest = len(SUMS), max(steps for _, steps, _ in SUMS)
+    return pl.pallas_call(
+        gather_kernel,
+        out_shape=(
+            piece, jax.ShapeDtypeStruct(slab.shape, BF16), jax.ShapeDtypeStruct((384, 128), BF16),
+            jax.ShapeDtypeStruct((128, 128), F32), jax.ShapeDtypeStruct((128, 128), BF16)),
+        in_specs=[pl.BlockSpec(memory_space=pltpu.SMEM), vmem, vmem, anyspace, anyspace, anyspace],
+        out_specs=(vmem,) * 5,
+        scratch_shapes=[
+            pltpu.VMEM((6, funcs, layers, rows_y, depth), BF16),
+            pltpu.VMEM((6, funcs, rows_y, depth), BF16),
+            pltpu.VMEM((subs, layers, rows_y, depth), jnp.int32),
+            pltpu.VMEM((subs, rows_y, depth), jnp.int32),
+            pltpu.VMEM((6, layers, 5, rows_y, depth), F32),
+            pltpu.VMEM((6, rows_y, depth), F32),
+            pltpu.VMEM((layers, funcs * rows_y, depth), F32),
+            pltpu.VMEM((funcs, rows_y * depth), BF16),
+            pltpu.VMEM((256, rows_y * depth), BF16),
+            pltpu.VMEM((6, funcs, rows_y * depth), BF16),
+            pltpu.VMEM((subs, funcs, 256), F32),
+            pltpu.VMEM((subs, 2 * funcs, 256), F32),
+            pltpu.VMEM((16, PIECE, 128), F32),
+            pltpu.VMEM((16, PIECE, 128), F32),
+            pltpu.VMEM((PIECE, 128), F32),
+            pltpu.VMEM((16, PIECE, 128), F32),
+            pltpu.VMEM((16, WIDER, 128), F32),
+            pltpu.VMEM((16, WIDER, 128), F32),
+            pltpu.VMEM((128, 128), F32),
+            pltpu.VMEM(slab.shape, BF16),
+            pltpu.VMEM((streams, longest, chunk, 128), BF16),
+            pltpu.VMEM((CHUNKS, chunk, 128), BF16),
+            pltpu.VMEM((CHUNKS, chunk, 128), BF16),
+            dma((6,)), dma((2,)), dma((6,)), dma((6,)), dma, dma,
+            dma((16,)), dma((16,)), dma((16,)), dma((16,)), dma((16,)), dma((16,)), dma((16,)), dma((16,)),
+            dma((streams, longest)), dma((streams, longest)), dma((CHUNKS,)), dma((CHUNKS,)), dma((streams, 4)), dma((streams, 4)),
+        ],
+        compiler_params=pltpu.CompilerParams(collective_id=0, has_side_effects=True, vmem_limit_bytes=63 << 20),
+        name="galerkin_gather",
+    )(owner, table, ids, basis, mat, slab)
+
+
+def panel_kernel(
+    owner_ref, own_ref, parts_ref, lower_ref, rows_ref, column_hbm, slab_hbm, out_hbm, galerkin_ref,
+    column, slab, out, block, column_sem, slab_sem, out_sem,
+):
+    w, n = lax.axis_index("wide"), lax.axis_index("narrow")
+    owner = owner_ref[0]
+    funcs = galerkin_ref.shape[1]
+    tile = out.shape[0] // TILES
+
+    def rows_of(t):
+        return pl.ds(pl.multiple_of(t * tile, tile), tile)
+
+    def column_load(t):
+        return pltpu.make_async_copy(column_hbm.at[rows_of(t)], column.at[rows_of(t)], column_sem.at[t])
+
+    def slab_load(t):
+        return pltpu.make_async_copy(slab_hbm.at[rows_of(t)], slab.at[rows_of(t)], slab_sem.at[t])
+
+    def out_store(t):
+        return pltpu.make_async_copy(out.at[rows_of(t)], out_hbm.at[rows_of(t)], out_sem.at[t])
+
+    for t in range(TILES):
+        column_load(t).start()
+        slab_load(t).start()
+    block[...] = jnp.zeros_like(block)
     for s in range(2):
-        for z in range(8):
-            galerkin_ref[s, 12 * z:12 * (z + 1), :] = own_ref[2 * z + s, 0:12, 0:funcs]
-    loads[2].wait()
-    loads[3].wait()
-    rows = jnp.concatenate([panel_ref[q, 24:32, :] for q in range(16)], 0)
-    rows_bf[...] = solve(rows.astype(BF16)).astype(BF16)
-    added_own[...] = jnp.zeros_like(added_own)
-
-    @pl.when((w == n) & (n >= owner))
-    def _():
-        added_own[...] = added_of(own_ref)
-
-    def store(start, size, factor, base):
-        part = pl.ds(start, size)
+        for part in range(RING):
+            galerkin_ref[s, 12 * part:12 * (part + 1), :] = own_ref[2 * part + s, 0:12, 0:funcs]
+
+    def store(t, factor):
+        part = rows_of(t)
 
         @pl.when(n > owner)
         def _():
-            update = lax.dot_general(factor, rows_bf[...], NT, preferred_element_type=F32)
-            out_ref[part, :] = (base - update).astype(BF16)
+            update = lax.dot_general(factor, rows_ref[...], NT, preferred_element_type=F32)
+            out[part, :] = (slab[part, :].astype(F32) - update).astype(BF16)
 
         @pl.when(n == owner)
         def _():
-            out_ref[part, :] = factor
+            out[part, :] = factor
 
         @pl.when(n < owner)
         def _():
-            out_ref[part, :] = base.astype(BF16)
-
-    solved = solve(column_ref[0:128, :])
-    solved = jnp.where(w == owner, lower[...], solved)
-    solved = jnp.where(w < owner, 0.0, solved)
-    store(0, 128, solved.astype(BF16), slab_ref[0:128, :].astype(F32) + added_own[...])
+            out[part, :] = slab[part, :]
+
+    column_load(0).wait()
+    slab_load(0).wait()
+    solved = solve(column[0:tile, :], parts_ref[...])
+    top = jnp.where(w == owner, lower_ref[...], solved[0:128])
+    top = jnp.where(w < owner, 0.0, top)
+    factor = jnp.concatenate([top, solved[128:tile]], 0).astype(BF16)
+    store(0, factor)
+
+    @pl.when((w == n) & (n > owner))
+    def _():
+        update = lax.dot_general(factor[0:128], rows_ref[...], NT, preferred_element_type=F32)
+        base = slab[0:128, :].astype(F32) + added_of(own_ref, block)
+        out[0:128, :] = (base - update).astype(BF16)
+
+    out_store(0).start()
 
     def body(t, carry):
-        start = pl.multiple_of(128 + t * tile, 128)
-        part = pl.ds(start, tile)
-        store(start, tile, solve(column_ref[part, :]).astype(BF16), slab_ref[part, :].astype(F32))
+        column_load(t).wait()
+        slab_load(t).wait()
+        store(t, solve(column[rows_of(t), :], parts_ref[...]).astype(BF16))
+        out_store(t).start()
         return carry
 
-    steps = (height - 128) // tile
-    lax.fori_loop(0, steps, body, 0)
-    done = 128 + steps * tile
-    rest = slice(done, height)
-    store(done, height - done, solve(column_ref[rest, :]).astype(BF16), slab_ref[rest, :].astype(F32))
-
-
-def panel_step(owner, panel, own, column, slab, funcs):
-    vmem = pl.BlockSpec(memory_space=pltpu.VMEM)
+    lax.fori_loop(1, TILES, body, 0)
+    for t in range(TILES):
+        out_store(t).wait()
+
+
+def panel_step(owner, own, column, parts, lower, rows, slab, funcs):
+    vmem, anyspace = pl.BlockSpec(memory_space=pltpu.VMEM), pl.BlockSpec(memory_space=pl.ANY)
+    dma = pltpu.SemaphoreType.DMA
     return pl.pallas_call(
         panel_kernel,
         out_shape=(jax.ShapeDtypeStruct(slab.shape, BF16), jax.ShapeDtypeStruct((2, funcs, funcs), F32)),
-        in_specs=[pl.BlockSpec(memory_space=pltpu.SMEM)] + [pl.BlockSpec(memory_space=pl.ANY)] * 4,
-        out_specs=(vmem, vmem),
+        in_specs=[pl.BlockSpec(memory_space=pltpu.SMEM), vmem, vmem, vmem, vmem, anyspace, anyspace],
+        out_specs=(anyspace, vmem),
         scratch_shapes=[
-            pltpu.VMEM(panel.shape, F32), pltpu.VMEM(own.shape, F32), pltpu.VMEM(slab.shape, BF16), pltpu.VMEM(slab.shape, BF16),
-            pltpu.VMEM((128, 128), F32), pltpu.VMEM((128, 128), F32), pltpu.VMEM((128, 128), F32),
-            pltpu.VMEM((384, 128), BF16), pltpu.VMEM((128, 128), BF16),
-            pltpu.SemaphoreType.DMA((4,)),
+            pltpu.VMEM(slab.shape, BF16), pltpu.VMEM(slab.shape, BF16), pltpu.VMEM(slab.shape, BF16),
+            pltpu.VMEM((128, 128), F32), dma((TILES,)), dma((TILES,)), dma((TILES,)),
         ],
         compiler_params=pltpu.CompilerParams(vmem_limit_bytes=63 << 20),
         name="panel_step",
-    )(owner, panel, own, column, slab)
+    )(owner, own, parts, lower, rows, column, slab)
 
 
 def on_device(coarse_basis, material_ids, lame_table, coarse_ids, coarse_slab, panel_owner):
-    own, panel, column = gather(panel_owner, lame_table, coarse_ids, coarse_basis, material_ids, coarse_slab)
-    return panel_step(panel_owner, panel, own, column, coarse_slab, coarse_basis.shape[1])
+    own, column, parts, lower, rows = gather(panel_owner, lame_table, coarse_ids, coarse_basis, material_ids, coarse_slab)
+    return panel_step(panel_owner, own, column, parts, lower, rows, coarse_slab, coarse_basis.shape[1])
 
 
 def solution(mesh):

time: 103 us -> 95.7 us (0.929)
  Pallas kernels: 100 us -> 92.5 us
    pallas_call x1, Pallas kernels: 17.5 us -> 6.26 us  [panel_step(): pl.pallas_call(panel_kernel, out_shape=(jax.ShapeDtypeStruct(slab.shape,...]
    pallas_call x1, Pallas kernels: 82.9 us -> 86.3 us  [gather(): pl.pallas_call(gather_kernel, out_shape=(piece, jax.ShapeDtypeStruct(slab...]
where the time goes in v5:
time: 95.7 us; the launch traced here: 93.8 us
  Pallas kernels  92.5 us (97%)
  between operations  1.29 us (1%)
    pallas_call x1, Pallas kernels, gather(): pl.pallas_call(gather_kernel, out_shape=(piece, jax.ShapeDtypeStruct(slab...  86.3 us
    pallas_call x1, Pallas kernels, panel_step(): pl.pallas_call(panel_kernel, out_shape=(jax.ShapeDtypeStruct(slab.shape,...  6.26 us

profile of v5, /device:TPU:32, one launch (start us, length us, event | category | flops | bytes accessed | tf_op | source)
XLA Modules:
  0.0 93.8 jit_solution(9026969342948501124)
XLA Ops:
  1.3 86.3 %galerkin_gather.1 = (f32[16,24,128]{2,1,0:T(8,128)}, bf16[6144,128]{1,0:T(8,128)(2,1)}, bf16[384,128]{1,0:T(8,128)(2,1)}, f32[128,128]{1,0:T(8,128)}, bf16[128,128]{1,0:T(8,128)(2,1)}) custom-call(s32[1]{0:T(128)S(6)} %copy.8.owner_ref, bf16[2,16]{1,0:T(2,128)(2,1)} %table_ref.1, s32[2,96]{1,0:T(2,128)} %ids_ref.1, ...), custom_call_target="tpu_custom_call" | custom-call | tf_op jit(solution)/shard_map/galerkin_gather/pallas_call | solution.py:410
  87.6 6.3 %panel_step.1 = (bf16[6144,128]{1,0:T(8,128)(2,1)}, f32[2,96,96]{2,1,0:T(8,128)}) custom-call(s32[1]{0:T(128)S(6)} %copy.8.owner_ref, f32[16,24,128]{2,1,0:T(8,128)} %get-tuple-element.7.own_ref, bf16[384,128]{1,0:T(8,128)(2,1)} %get-tuple-element.8.parts_ref, f32[128,128]{1,0:T(8,128)} %get-tuple-element.9.lower_ref, ...), custom_call_target="tpu_custom_call" | custom-call | tf_op jit(solution)/shard_map/panel_step/pallas_call | solution.py:526

commit v6 on v5

--- a/solution.py
+++ b/solution.py
@@ -16,7 +16,7 @@
 RING = 8
 TILES = 8
 CHUNKS = 2
-SUMS = ((-1, 6, 0), (-1, 6, 1), (1, 1, 0), (1, 1, 1))
+SUMS = ((-1, 4, 0), (-1, 4, 1), (1, 3, 0), (1, 3, 1))
 SPREAD = ((-1, 4, 0), (-1, 4, 1), (1, 3, 0), (1, 3, 1))
 
 
@@ -79,14 +79,15 @@
     def halo_copy(sc):
         s, c = lax.div(sc, 3), lax.rem(sc, 3)
         return pltpu.make_async_remote_copy(
-            src_ref=basis_ref.at[s, :, c, layers - 1], dst_ref=halo.at[sc],
+            src_ref=basis_ref.at[s, :, c, (layers - 1) * (1 - s)], dst_ref=halo.at[sc],
             send_sem=halo_send.at[sc], recv_sem=halo_recv.at[sc],
-            device_id=(w, group(1)), device_id_type=MESH)
+            device_id=(w, group(1 + (count - 2) * s)), device_id_type=MESH)
 
     z, half = lax.div(n, 2), lax.rem(n, 2)
     piece_rows = column_ref.shape[0] // RING
     chunk = piece_rows // CHUNKS
     ring = lambda shift: lax.rem(z + shift + RING, RING)
+    flip = 2 * half - 1
     beside = lambda way: 2 * ring(way) + half
 
     def chunk_rows(c, piece):
@@ -96,14 +97,16 @@
         return pltpu.make_async_remote_copy(
             src_ref=passing.at[t, k - 1] if source is None else source, dst_ref=passing.at[t, k],
             send_sem=ring_send.at[t, k], recv_sem=ring_recv.at[t, k],
-            device_id=(w, beside(SUMS[t][0])), device_id_type=MESH)
+            device_id=(w, beside(SUMS[t][0] * flip)), device_id_type=MESH)
 
     def ring_start(t):
         way, steps, c = SUMS[t]
+        way = way * flip
         ring_copy(t, 0, masked.at[chunk_rows(c, ring(way * steps))]).start()
 
     def ring_step(t, k, last):
         way, steps, c = SUMS[t]
+        way = way * flip
         ring_copy(t, k, passing.at[t, k]).wait()
         if not last:
             passing[t, k] += masked[chunk_rows(c, ring(way * (steps - 1 - k))), :]
@@ -134,9 +137,10 @@
 
     mat_copy = pltpu.make_async_copy(mat_ref, mats, small_sem.at[0])
     slab_copy = pltpu.make_async_copy(slab_ref, masked, small_sem.at[1])
-    mat_halo_copy = pltpu.make_async_remote_copy(
-        src_ref=mat_ref.at[:, layers - 1], dst_ref=mat_halo, send_sem=mat_send, recv_sem=mat_recv,
-        device_id=(w, group(1)), device_id_type=MESH)
+    def mat_halo_copy(s):
+        return pltpu.make_async_remote_copy(
+            src_ref=mat_ref.at[s, (layers - 1) * (1 - s)], dst_ref=mat_halo.at[s], send_sem=mat_send.at[s], recv_sem=mat_recv.at[s],
+            device_id=(w, group(1 + (count - 2) * s)), device_id_type=MESH)
 
     slab_copy.start()
     mat_copy.start()
@@ -162,7 +166,8 @@
     lax.fori_loop(0, RING, mask, 0)
     pl.semaphore_wait(barrier, 2 * (count - 1))
 
-    mat_halo_copy.start()
+    for s in range(2):
+        mat_halo_copy(s).start()
     for t in range(len(SUMS)):
         ring_start(t)
     for sc in range(2):
@@ -175,8 +180,9 @@
 
     table = table_ref[...].astype(F32)
     mat_copy.wait()
-    mat_halo_copy.wait()
-    bottom = jnp.where(n == 0, 0.0, 1.0)
+    for s in range(2):
+        mat_halo_copy(s).wait()
+    bottom = jnp.where(n == 0, 1.0, 0.0)
     top = jnp.where(n == count - 1, 1.0, 0.0)
 
     def lame(material):
@@ -189,21 +195,22 @@
         return shear, dilate
 
     for s in range(2):
-        below = [x * bottom for x in lame(mat_halo[s])]
+        present = 1.0 - (bottom, top)[s]
+        edge, far = (layers - 1) * s, (top, bottom)[s]
+        outer = [x * present for x in lame(mat_halo[s])]
         cells = [lame(mats[s, i]) for i in range(layers)]
         for i in range(layers):
             here = cells[i]
-            lower_x = below if i == 0 else cells[i - 1]
 
             def weights(other):
                 m = 0.5 * (here[0] + other[0])
                 return m, m + (m + 0.5 * (here[1] + other[1]))
 
-            x_low = weights(lower_x)
-            if i + 1 < layers:
-                x_high = weights(cells[i + 1])
-            else:
-                x_high = [x * top for x in weights((jnp.zeros_like(here[0]),) * 2)]
+            def outside(owned):
+                return weights(outer) if owned else [x * far for x in weights((jnp.zeros_like(here[0]),) * 2)]
+
+            x_low = weights(cells[i - 1]) if i > 0 else outside(s == 0)
+            x_high = weights(cells[i + 1]) if i + 1 < layers else outside(s == 1)
             y_low = weights([shift_up(x, 0) for x in here])
             y_high = weights([shift_down(x, 0) for x in here])
             z_low = weights([shift_up(x, 1) for x in here])
@@ -216,8 +223,8 @@
                 coef[3 * s + c, i, 2] = y_low[py]
                 coef[3 * s + c, i, 3] = jnp.where(lane == 0, 0.0, z_low[pz])
                 coef[3 * s + c, i, 4] = jnp.where(lane == lane.shape[1] - 1, 0.0, z_high[pz])
-                if i == 0:
-                    coef_halo[3 * s + c] = x_low[px] * bottom
+                if i == edge:
+                    coef_halo[3 * s + c] = (x_low, x_high)[s][px] * present
 
     rows_y = 8
 
@@ -250,10 +257,14 @@
                 hi, lo = split2(image)
                 vb = v.astype(BF16)
                 left[:, lanes] = vb
-                if i == 0:
-                    first[sc, :, lanes] = vb
                 right[0:funcs, lanes] = hi
                 right[128:128 + funcs, lanes] = lo
+            if i in (0, layers - 1):
+
+                @pl.when(s == i // (layers - 1))
+                def _():
+                    first[sc] = left[...]
+
             acc[s] += lax.dot_general(left[...], right[...], NT, preferred_element_type=F32)
         halo_copy(sc).wait_send()
 
@@ -261,9 +272,14 @@
         def _():
             halo_copy(sc + 2).start()
 
-        @pl.when(sc >= 1)
+        @pl.when((sc >= 1) & (sc <= 3))
         def _():
             for t in range(CHUNKS):
+                ring_step(t, sc - 1, False)
+
+        @pl.when((sc == 1) | (sc == 2))
+        def _():
+            for t in range(CHUNKS, 2 * CHUNKS):
                 ring_step(t, sc - 1, False)
 
         return carry
@@ -284,6 +300,10 @@
         late[s, funcs:2 * funcs] += lax.dot_general(first[sc], right[...], NT, preferred_element_type=F32)
         return carry
 
+    for c in range(CHUNKS):
+        ring_step(c, SUMS[0][1] - 1, True)
+        ring_step(CHUNKS + c, SUMS[2][1] - 1, True)
+        swap_start(c)
     lax.fori_loop(0, 6, boundary, 0)
 
     head = masked[0:128, :].astype(F32)
@@ -327,9 +347,10 @@
     start_all(rs_copy)
     landed[n] = pieces[n]
     for c in range(CHUNKS):
-        ring_step(c, SUMS[0][1] - 1, True)
-        ring_step(CHUNKS + c, 0, True)
-        swap_start(c)
+        swap_copy(c).wait()
+        column_ref[chunk_rows(c, z), :] = settled[c] + swapped[c]
+        for t in (c, CHUNKS + c):
+            spread_copy(t, 0).start()
     wait_all(rs_copy)
     total = landed[0]
     for q in range(1, 16):
@@ -341,11 +362,7 @@
     start_all(own_copy)
     own_ref[n] = reduced[...]
     wide_in[w] = reduced[...]
-    for c in range(CHUNKS):
-        swap_copy(c).wait()
-        column_ref[chunk_rows(c, z), :] = settled[c] + swapped[c]
-        for t in (c, CHUNKS + c):
-            spread_copy(t, 0).start()
+    spread_step(0)
     wait_all(wide_copy)
     of_owner = wide_in[owner_ref[0]]
     for q in range(16):
@@ -354,7 +371,6 @@
     start_all(panel_copy)
     panel_ref[n] = chosen[n]
     block[...] = jnp.zeros_like(block)
-    spread_step(0)
     spread_step(1)
     wait_all(panel_copy)
 
@@ -438,7 +454,7 @@
             pltpu.VMEM((streams, longest, chunk, 128), BF16),
             pltpu.VMEM((CHUNKS, chunk, 128), BF16),
             pltpu.VMEM((CHUNKS, chunk, 128), BF16),
-            dma((6,)), dma((2,)), dma((6,)), dma((6,)), dma, dma,
+            dma((6,)), dma((2,)), dma((6,)), dma((6,)), dma((2,)), dma((2,)),
             dma((16,)), dma((16,)), dma((16,)), dma((16,)), dma((16,)), dma((16,)), dma((16,)), dma((16,)),
             dma((streams, longest)), dma((streams, longest)), dma((CHUNKS,)), dma((CHUNKS,)), dma((streams, 4)), dma((streams, 4)),
         ],

time: 95.7 us -> 93.2 us (0.974)
  Pallas kernels: 92.5 us -> 90.6 us
    pallas_call x1, Pallas kernels: 86.3 us -> 84.3 us  [gather(): pl.pallas_call(gather_kernel, out_shape=(piece, jax.ShapeDtypeStruct(slab...]
where the time goes in v6:
time: 93.2 us; the launch traced here: 91.9 us
  Pallas kernels  90.6 us (97%)
  between operations  1.29 us (1%)
    pallas_call x1, Pallas kernels, gather(): pl.pallas_call(gather_kernel, out_shape=(piece, jax.ShapeDtypeStruct(slab...  84.3 us
    pallas_call x1, Pallas kernels, panel_step(): pl.pallas_call(panel_kernel, out_shape=(jax.ShapeDtypeStruct(slab.shape,...  6.29 us

profile of v6, /device:TPU:32, one launch (start us, length us, event | category | flops | bytes accessed | tf_op | source)
XLA Modules:
  0.0 91.9 jit_solution(11045470921927349074)
XLA Ops:
  1.3 84.3 %galerkin_gather.1 = (f32[16,24,128]{2,1,0:T(8,128)}, bf16[6144,128]{1,0:T(8,128)(2,1)}, bf16[384,128]{1,0:T(8,128)(2,1)}, f32[128,128]{1,0:T(8,128)}, bf16[128,128]{1,0:T(8,128)(2,1)}) custom-call(s32[1]{0:T(128)S(6)} %copy.8.owner_ref, bf16[2,16]{1,0:T(2,128)(2,1)} %table_ref.1, s32[2,96]{1,0:T(2,128)} %ids_ref.1, ...), custom_call_target="tpu_custom_call" | custom-call | tf_op jit(solution)/shard_map/galerkin_gather/pallas_call | solution.py:426
  85.6 6.3 %panel_step.1 = (bf16[6144,128]{1,0:T(8,128)(2,1)}, f32[2,96,96]{2,1,0:T(8,128)}) custom-call(s32[1]{0:T(128)S(6)} %copy.8.owner_ref, f32[16,24,128]{2,1,0:T(8,128)} %get-tuple-element.7.own_ref, bf16[384,128]{1,0:T(8,128)(2,1)} %get-tuple-element.8.parts_ref, f32[128,128]{1,0:T(8,128)} %get-tuple-element.9.lower_ref, ...), custom_call_target="tpu_custom_call" | custom-call | tf_op jit(solution)/shard_map/panel_step/pallas_call | solution.py:542

commit v7 on v6

--- a/solution.py
+++ b/solution.py
@@ -170,8 +170,7 @@
         mat_halo_copy(s).start()
     for t in range(len(SUMS)):
         ring_start(t)
-    for sc in range(2):
-        halo_copy(sc).start()
+    halo_copy(0).start()
 
     acc[...] = jnp.zeros_like(acc)
     late[...] = jnp.zeros_like(late)
@@ -268,9 +267,9 @@
             acc[s] += lax.dot_general(left[...], right[...], NT, preferred_element_type=F32)
         halo_copy(sc).wait_send()
 
-        @pl.when(sc < 4)
+        @pl.when(sc < 5)
         def _():
-            halo_copy(sc + 2).start()
+            halo_copy(sc + 1).start()
 
         @pl.when((sc >= 1) & (sc <= 3))
         def _():

time: 93.2 us -> 99.6 us (1.069)
  the two profiles are of different devices: /device:TPU:32 before, /device:TPU:4 now
where the time goes in v7:
time: 99.6 us; the launch traced here: 99.4 us
  Pallas kernels  98.1 us (98%)
  between operations  1.29 us (1%)
    pallas_call x1, Pallas kernels, gather(): pl.pallas_call(gather_kernel, out_shape=(piece, jax.ShapeDtypeStruct(slab...  91.9 us
    pallas_call x1, Pallas kernels, panel_step(): pl.pallas_call(panel_kernel, out_shape=(jax.ShapeDtypeStruct(slab.shape,...  6.28 us

profile of v7, /device:TPU:4, one launch (start us, length us, event | category | flops | bytes accessed | tf_op | source)
XLA Modules:
  0.0 99.4 jit_solution(16149189960874616365)
XLA Ops:
  1.3 91.9 %galerkin_gather.1 = (f32[16,24,128]{2,1,0:T(8,128)}, bf16[6144,128]{1,0:T(8,128)(2,1)}, bf16[384,128]{1,0:T(8,128)(2,1)}, f32[128,128]{1,0:T(8,128)}, bf16[128,128]{1,0:T(8,128)(2,1)}) custom-call(s32[1]{0:T(128)S(6)} %copy.8.owner_ref, bf16[2,16]{1,0:T(2,128)(2,1)} %table_ref.1, s32[2,96]{1,0:T(2,128)} %ids_ref.1, ...), custom_call_target="tpu_custom_call" | custom-call | tf_op jit(solution)/shard_map/galerkin_gather/pallas_call | solution.py:425
  93.1 6.3 %panel_step.1 = (bf16[6144,128]{1,0:T(8,128)(2,1)}, f32[2,96,96]{2,1,0:T(8,128)}) custom-call(s32[1]{0:T(128)S(6)} %copy.8.owner_ref, f32[16,24,128]{2,1,0:T(8,128)} %get-tuple-element.7.own_ref, bf16[384,128]{1,0:T(8,128)(2,1)} %get-tuple-element.8.parts_ref, f32[128,128]{1,0:T(8,128)} %get-tuple-element.9.lower_ref, ...), custom_call_target="tpu_custom_call" | custom-call | tf_op jit(solution)/shard_map/panel_step/pallas_call | solution.py:541
